TPU v7x, 32 devices: a whole 2x2x4 slice. The times are simulated.
32 devices in a mesh: vol: 2 (over x), gz: 16 (over z, y, core).
Axes of the slice: x: 2, y: 2, z: 4, core: 2. Of those that a mesh axis runs over, the one named last changes fastest.
Arguments:
- tomogram: float32 [64, 32, 128], P(('vol', 'gz')), parts along dimension 0, may hold values from -120 to 120
- initial_maps: bfloat16 [32, 64, 32, 128], P(None, ('vol', 'gz')), parts along dimension 1, may hold values from -7.2 to 7.2
- dictionary: float32 [32, 64], replicated, may hold values from -0.75 to 0.75
- thresholds: float32 [32], replicated, may hold values from 0.05 to 0.5
Outputs:
- sparse_maps: bfloat16 [32, 64, 32, 128], P(None, ('vol', 'gz')), parts along dimension 1
- descent: float32 [64, 64], P('vol'), parts along dimension 0
- curvature: float32 [2], P('vol'), parts along dimension 0
- residual: float32 [64, 32, 128], P(('vol', 'gz')), parts along dimension 0
There are 2 independent parts, one for each index of `vol`. A program takes and returns all parts, laid end to end along the dimension named above; an argument that names none is the same for every part. Nothing has to cross between parts.
All inputs are finite; a program needn't handle non-finite values.
Results may differ from a plain program's by a relative error of at most 0.012.
Values may be sent and summed in bfloat16 or wider, within the bound.
No kernel may reach another device: no remote copies, remote signals or barrier semaphores. Data moves between devices by JAX's collectives and lax.ppermute only.
A program may use at most 64 MiB of HBM per device.

v0:
```python
import functools
import math

import jax
import jax.numpy as jnp
from jax import lax
from jax.experimental import pallas as pl
from jax.experimental.pallas import tpu as pltpu
from jax.sharding import PartitionSpec as P

coef_step = 0.015
second_t = (1.0 + math.sqrt(5.0)) / 2.0
third_t = (1.0 + math.sqrt(1.0 + 4.0 * second_t * second_t)) / 2.0
momentum = (second_t - 1.0) / third_t

F32 = jnp.float32
BF16 = jnp.bfloat16
CHUNK = 512


def iota(shape, dim):
    return lax.broadcasted_iota(jnp.int32, shape, dim)


def tap_select(slab, plane, shape, tap_dim):
    tap, col = iota(shape, tap_dim), iota(shape, 1 - tap_dim)
    lands = (2 * slab + plane - 1 + (tap >> 4)) & 7
    return (((tap & 15) == (col >> 3)) & (lands == (col & 7))).astype(BF16)


def taps_dot(lhs, rhs, dims):
    return lax.dot_general(lhs, rhs, (dims, ((), ())), preferred_element_type=F32)


def bank_rows(atoms, slab):
    parts = [taps_dot(atoms, tap_select(slab, z, (64, 128), 0), ((1,), (0,))) for z in range(2)]
    return jnp.concatenate(parts, axis=0).astype(BF16)


def bank_cols(atoms, slab):
    parts = [taps_dot(tap_select(slab, z, (128, 64), 1), atoms, ((1,), (1,))) for z in range(2)]
    return jnp.concatenate(parts, axis=1).astype(BF16)


def spread(bank, maps, products, height, breadth, emit):
    zeros = jnp.zeros((128, 2 * breadth), F32)
    size = height * breadth
    products[:, : 2 * breadth] = zeros
    products[:, 2 * breadth + size :] = zeros[:, :breadth]
    for start in range(0, size, CHUNK):
        products[:, 2 * breadth + start : 2 * breadth + start + CHUNK] = jnp.dot(
            bank, maps[:, start : start + CHUNK], preferred_element_type=F32
        )
    lane = iota((8, breadth), 1)
    for y in range(height):
        sums = []
        for col in range(4):
            terms = [
                products[
                    (4 * row + col) * 8 : (4 * row + col) * 8 + 8,
                    (y + 3 - row) * breadth : (y + 4 - row) * breadth,
                ]
                for row in range(4)
            ]
            sums.append((terms[0] + terms[1]) + (terms[2] + terms[3]))
        total = sums[1] + jnp.where(lane < breadth - 1, pltpu.roll(sums[0], breadth - 1, 1), 0.0)
        total += jnp.where(lane >= 1, pltpu.roll(sums[2], 1, 1), 0.0)
        total += jnp.where(lane >= 2, pltpu.roll(sums[3], 2, 1), 0.0)
        emit(y, total)


def emit_share(slab, tomo, share, height, breadth):
    row = iota((8, breadth), 0)
    first, second = row == ((2 * slab) & 7), row == ((2 * slab + 1) & 7)

    def emit(y, total):
        own = jnp.where(first, tomo[y : y + 1, :], jnp.where(second, tomo[height + y : height + y + 1, :], 0.0))
        share[:, y * breadth : (y + 1) * breadth] = own - total

    return emit


def plane_offset(slab, shape):
    return (iota(shape, 0) - (2 * slab - 1)) & 7


def sent_range(slab, offset):
    low = 2 * (slab & 1)
    return (offset >= low) & (offset <= low + 2)


def gather_resid(slab, slabs, mine, mate, beside, relayed, height, breadth, visit):
    offset = plane_offset(slab, (8, breadth))
    from_beside = sent_range(slab, offset)
    from_relay = offset == 4 * (1 - (slab & 1))
    plane = 2 * slab - 1 + offset
    valid = (offset < 5) & (plane >= 0) & (plane < 2 * slabs)
    for y in range(height):
        cols = slice(y * breadth, (y + 1) * breadth)
        near, far = beside[:, cols], relayed[:, cols]
        total = mine[:, cols] + mate[:, cols]
        total += jnp.where(from_beside, jnp.concatenate([near, near], axis=0), 0.0)
        total += jnp.where(from_relay, jnp.concatenate([far, far], axis=0), 0.0)
        visit(y, jnp.where(valid, total, 0.0))


def unfold(resid, unfolded, height, breadth, y):
    lane = iota((8, breadth), 1)
    shifted = [
        jnp.where(lane >= 1, pltpu.roll(resid, 1, 1), 0.0),
        resid,
        jnp.where(lane < breadth - 1, pltpu.roll(resid, breadth - 1, 1), 0.0),
        jnp.where(lane < breadth - 2, pltpu.roll(resid, breadth - 2, 1), 0.0),
    ]
    halves = [jnp.concatenate(shifted[k : k + 2], axis=0).astype(BF16) for k in (0, 2)]
    for row in range(4):
        target = y - row + 1
        if 0 <= target < height:
            for k in range(2):
                start = row * 32 + k * 16
                unfolded[start : start + 16, target * breadth : (target + 1) * breadth] = halves[k]


def unfold_edges(unfolded, height, breadth):
    zeros = jnp.zeros((32, breadth), BF16)
    for row in range(4):
        for y in range(height):
            if not 0 <= y + row - 1 < height:
                unfolded[row * 32 : row * 32 + 32, y * breadth : (y + 1) * breadth] = zeros


def start_kernel(height, breadth, slab_ref, maps, tomo, atoms, share, by_voxel, rows_out, cols_out, wide, products):
    slab = slab_ref[0]
    atom_count = by_voxel.shape[0] // 2
    bank = atoms[...].astype(BF16)
    rows_out[...] = bank_rows(bank, slab)
    cols = bank_cols(bank, slab)
    cols_out[...] = cols
    wide[...] = maps[...].astype(F32)
    for y in range(height):
        for z in range(2):
            part = wide[pl.ds(z * height + y, atom_count, stride=2 * height), :]
            by_voxel[z * atom_count : (z + 1) * atom_count, y * breadth : (y + 1) * breadth] = part.astype(BF16)
    spread(cols, by_voxel, products, height, breadth, emit_share(slab, tomo, share, height, breadth))


def relay_kernel(slab_ref, mine, mate, out):
    slab = slab_ref[0]
    total = mine[...] + mate[...]
    total = jnp.where(sent_range(slab, plane_offset(slab, total.shape)), total, 0.0)
    out[...] = total[:4] + total[4:]


def step_kernel(height, breadth, slabs, last, slab_ref, mine, mate, beside, relayed, maps, tomo, rows, cols, limits, *rest):
    if last:
        share, by_voxel, natural, unfolded, products, wide = rest
    else:
        share, by_voxel, unfolded, products = rest
    slab = slab_ref[0]
    size = height * breadth
    atom_count = maps.shape[0] // 2
    unfold_edges(unfolded, height, breadth)
    gather_resid(
        slab, slabs, mine, mate, beside, relayed, height, breadth,
        lambda y, resid: unfold(resid, unfolded, height, breadth, y),
    )
    square = (atom_count, atom_count)
    column = jnp.sum(jnp.where(iota(square, 0) == iota(square, 1), limits[...], 0.0), axis=1, keepdims=True)
    limit = jnp.concatenate([column, column], axis=0)
    bank = rows[...]
    for start in range(0, size, CHUNK):
        part = slice(start, start + CHUNK)
        gradient = jnp.dot(bank, unfolded[:, part], preferred_element_type=F32)
        before = maps[:, part].astype(F32)
        moved = before - coef_step * gradient
        after = moved - jnp.clip(moved, -limit, limit)
        if last:
            by_voxel[:, part] = after.astype(BF16)
            for k in range(CHUNK // breadth):
                y = start // breadth + k
                for z in range(2):
                    wide[pl.ds(z * height + y, atom_count, stride=2 * height), :] = after[
                        z * atom_count : (z + 1) * atom_count, k * breadth : (k + 1) * breadth
                    ]
        else:
            after = after.astype(BF16).astype(F32)
            by_voxel[:, part] = (after + momentum * (after - before)).astype(BF16)
    spread(cols[...], by_voxel, products, height, breadth, emit_share(slab, tomo, share, height, breadth))
    if last:
        natural[...] = wide[...].astype(BF16)


def descent_kernel(height, breadth, slabs, slab_ref, mine, mate, beside, relayed, maps, shares, resid_out, unfolded, planes):
    slab = slab_ref[0]
    atom_count = maps.shape[0] // 2
    unfold_edges(unfolded, height, breadth)

    def visit(y, resid):
        planes[8 * y : 8 * y + 8, :] = resid
        unfold(resid, unfolded, height, breadth, y)

    gather_resid(slab, slabs, mine, mate, beside, relayed, height, breadth, visit)
    for z in range(2):
        resid_out[z * height : (z + 1) * height, :] = planes[pl.ds((2 * slab + z) & 7, height, stride=8), :]
    both = taps_dot(maps[...], unfolded[...], ((1,), (1,)))
    total = jnp.zeros((atom_count, 64), F32)
    for z in range(2):
        left = both[z * atom_count : (z + 1) * atom_count, :]
        pick = tap_select(slab, z, (128, 64), 1)
        for _ in range(3):
            head = left.astype(BF16)
            total += taps_dot(head, pick, ((1,), (0,)))
            left = left - head.astype(F32)
    half = atom_count // 2
    packed = jnp.concatenate([total[:half], total[half:]], axis=1)
    for j in range(slabs):
        shares[j] = packed


def probe_kernel(height, breadth, slab_ref, shares, maps, descent_out, share, send, products):
    slab = slab_ref[0]
    packed = jnp.sum(shares[...], axis=0)
    descent = jnp.concatenate([packed[:, :64], packed[:, 64:]], axis=0)
    descent_out[...] = descent

    def emit(y, total):
        share[:, y * breadth : (y + 1) * breadth] = total

    spread(bank_cols(descent.astype(BF16), slab), maps, products, height, breadth, emit)
    total = share[...]
    total = jnp.where(sent_range(slab, plane_offset(slab, total.shape)), total, 0.0)
    send[...] = total[:4] + total[4:]


def square_kernel(slabs, slab_ref, mine, mate, beside, out):
    slab = slab_ref[0]
    offset = plane_offset(slab, mine.shape)
    near = beside[...]
    total = mine[...] + mate[...] + jnp.where(sent_range(slab, offset), jnp.concatenate([near, near], axis=0), 0.0)
    total = jnp.where((offset == 1) | (offset == 2), total * total, 0.0)
    folded = jnp.sum(total, axis=1, keepdims=True)
    out[...] = jnp.broadcast_to(jnp.sum(folded, axis=0, keepdims=True), out.shape)


def call(kernel, outs, operands, scratch=()):
    in_specs = [pl.BlockSpec(memory_space=pltpu.SMEM)] + [pl.BlockSpec(memory_space=pltpu.VMEM)] * (len(operands) - 1)
    return pl.pallas_call(
        kernel,
        out_shape=[jax.ShapeDtypeStruct(shape, dtype) for shape, dtype in outs],
        in_specs=in_specs,
        out_specs=[pl.BlockSpec(memory_space=pltpu.VMEM)] * len(outs),
        scratch_shapes=[pltpu.VMEM(shape, dtype) for shape, dtype in scratch],
    )(*operands)


def per_device(tomogram, initial_maps, dictionary, thresholds):
    slabs = lax.axis_size("gz")
    planes, height, breadth = tomogram.shape
    atom_count = initial_maps.shape[0]
    size = height * breadth
    slab = lax.axis_index("gz").astype(jnp.int32).reshape(1)
    tomo = tomogram.reshape(planes * height, breadth)
    natural = initial_maps.reshape(atom_count * planes * height, breadth)
    limits = thresholds.reshape(1, atom_count)

    mates = [(i, i ^ 1) for i in range(slabs)]
    besides = [(i, i + 1) for i in range(1, slabs - 1, 2)]
    besides += [(j, i) for i, j in besides]

    def to_mate(x):
        return lax.ppermute(x, "gz", mates)

    def to_beside(x):
        return lax.ppermute(x, "gz", besides)

    share_shape = ((8, size), F32)
    maps_shape = ((2 * atom_count, size), BF16)
    products = ((128, size + 3 * breadth), F32)
    unfolded = ((128, size), BF16)
    wide = ((2 * atom_count * height, breadth), F32)
    relay_shape = ((4, size), F32)

    def meet(mine):
        mate = to_mate(mine)
        (send,) = call(relay_kernel, [relay_shape], (slab, mine, mate))
        beside = to_beside(send)
        relayed = to_mate(beside)
        return mine, mate, beside, relayed

    share, maps, rows, cols = call(
        functools.partial(start_kernel, height, breadth),
        [share_shape, maps_shape, ((2 * atom_count, 128), BF16), ((128, 2 * atom_count), BF16)],
        (slab, natural, tomo, dictionary),
        [wide, products],
    )
    share, maps = call(
        functools.partial(step_kernel, height, breadth, slabs, False),
        [share_shape, maps_shape],
        (slab, *meet(share), maps, tomo, rows, cols, limits),
        [unfolded, products],
    )
    share, maps, natural = call(
        functools.partial(step_kernel, height, breadth, slabs, True),
        [share_shape, maps_shape, ((2 * atom_count * height, breadth), BF16)],
        (slab, *meet(share), maps, tomo, rows, cols, limits),
        [unfolded, products, wide],
    )
    shares, residual = call(
        functools.partial(descent_kernel, height, breadth, slabs),
        [((slabs, atom_count // 2, 128), F32), ((planes * height, breadth), F32)],
        (slab, *meet(share), maps),
        [unfolded, ((8 * height, breadth), F32)],
    )
    shares = lax.all_to_all(shares, "gz", 0, 0)
    descent, share, send = call(
        functools.partial(probe_kernel, height, breadth),
        [((atom_count, 64), F32), share_shape, relay_shape],
        (slab, shares, maps),
        [products],
    )
    (norms,) = call(
        functools.partial(square_kernel, slabs),
        [((slabs, 128), F32)],
        (slab, share, to_mate(share), to_beside(send)),
    )
    norms = lax.all_to_all(norms.reshape(slabs, 1, 128), "gz", 0, 0)
    curvature = jnp.sum(norms[:, :, :1]).reshape(1)
    return (
        natural.reshape(initial_maps.shape),
        descent,
        curvature,
        residual.reshape(tomogram.shape),
    )


def solution(mesh):
    return jax.shard_map(
        per_device,
        mesh=mesh,
        in_specs=(P(("vol", "gz"), None, None), P(None, ("vol", "gz"), None, None), P(), P()),
        out_specs=(
            P(None, ("vol", "gz"), None, None),
            P("vol", None),
            P("vol"),
            P(("vol", "gz"), None, None),
        ),
        check_vma=False,
    )
```

profile of v0, /device:TPU:0, one launch (start us, length us, event | category | flops | bytes accessed | tf_op | source)
XLA Modules:
  0.0 86.4 jit_solution(7683397984460922718)
XLA Ops:
  0.6 2.9 %shard_map.75 = (f32[8,4096]{1,0:T(8,128)}, bf16[64,4096]{1,0:T(8,128)(2,1)}, bf16[64,128]{1,0:T(8,128)(2,1)}, bf16[128,64]{1,0:T(8,128)(2,1)}) custom-call(s32[1]{0:T(128)} %bitcast.slab_ref, bf16[2048,128]{1,0:T(8,128)(2,1)} %bitcast.10, f32[64,128]{1,0:T(8,128)} %bitcast.11, f32[32,64]{1,0:T(8,128)} %atoms.1), custom_call_target="tpu_custom_call" | custom-call | tf_op jit(solution)/shard_map/pallas_call | solution.py:247
  3.5 0.5 collective-permute-start
  4.0 1.2 %collective-permute-done.mate = f32[8,4096]{1,0:T(8,128)S(1)} collective-permute-done((f32[8,4096]{1,0:T(8,128)}, f32[8,4096]{1,0:T(8,128)S(1)}, u32[]{:S(2)}, u32[]{:S(2)}) %collective-permute-start) | collective-permute-done | bytes 131104 | tf_op jit(solution)/shard_map/ppermute | solution.py:271
  5.2 0.6 copy-done.1
  5.8 1.6 %shard_map.76 = f32[4,4096]{1,0:T(4,128)} custom-call(s32[1]{0:T(128)} %bitcast.slab_ref, f32[8,4096]{1,0:T(8,128)} %get-tuple-element.18.mine, f32[8,4096]{1,0:T(8,128)} %copy-done.1), custom_call_target="tpu_custom_call" | custom-call | tf_op jit(solution)/shard_map/pallas_call | solution.py:247
  7.5 0.7 collective-permute-start.1
  8.1 0.0 collective-permute-done.1.beside
  8.2 0.0 copy-start.5
  8.2 6.4 %collective-permute-start.2 = (f32[4,4096]{1,0:T(4,128)S(1)}, f32[4,4096]{1,0:T(4,128)S(1)}, u32[]{:S(2)}, u32[]{:S(2)}) collective-permute-start(f32[4,4096]{1,0:T(4,128)S(1)} %collective-permute-done.1.beside), channel_id=1, source_target_pairs={{0,1},{1,0},{2,3},{3,2},{4,5},{5,4},{6,7},{7,6},{8,9},{9,8},{10,11... | collective-permute-start | bytes 196616 | tf_op jit(solution)/shard_map/ppermute | solution.py:271
  14.5 0.9 %collective-permute-done.2.relayed = f32[4,4096]{1,0:T(4,128)S(1)} collective-permute-done((f32[4,4096]{1,0:T(4,128)S(1)}, f32[4,4096]{1,0:T(4,128)S(1)}, u32[]{:S(2)}, u32[]{:S(2)}) %collective-permute-start.2) | collective-permute-done | bytes 65568 | tf_op jit(solution)/shard_map/ppermute | solution.py:271
  15.4 0.0 copy-done.5
  15.4 0.6 copy-done.8
  16.0 3.0 %shard_map.77 = (f32[8,4096]{1,0:T(8,128)}, bf16[64,4096]{1,0:T(8,128)(2,1)}) custom-call(s32[1]{0:T(128)} %bitcast.slab_ref, f32[8,4096]{1,0:T(8,128)} %get-tuple-element.18.mine, f32[8,4096]{1,0:T(8,128)} %copy-done.1, f32[4,4096]{1,0:T(4,128)} %copy-done.5, f32[4,4096]{1,0:T(4,128)} %copy-done.8, bf16[64,4096]{1,0:T(8,128)(2,1)} %get-tuple-element.19.maps, ...), custom_call_target="tpu_custom_call" | custom-call | tf_op jit(solution)/shard_map/pallas_call | solution.py:247
  19.0 0.4 collective-permute-start.3
  19.4 1.2 %collective-permute-done.3.mate = f32[8,4096]{1,0:T(8,128)S(1)} collective-permute-done((f32[8,4096]{1,0:T(8,128)}, f32[8,4096]{1,0:T(8,128)S(1)}, u32[]{:S(2)}, u32[]{:S(2)}) %collective-permute-start.3) | collective-permute-done | bytes 131104 | tf_op jit(solution)/shard_map/ppermute | solution.py:271
  20.6 0.7 copy-done
  21.2 1.6 %shard_map.78 = f32[4,4096]{1,0:T(4,128)} custom-call(s32[1]{0:T(128)} %bitcast.slab_ref, f32[8,4096]{1,0:T(8,128)} %get-tuple-element.22.mine, f32[8,4096]{1,0:T(8,128)} %copy-done), custom_call_target="tpu_custom_call" | custom-call | tf_op jit(solution)/shard_map/pallas_call | solution.py:247
  22.9 0.7 collective-permute-start.4
  23.5 0.0 collective-permute-done.4.beside
  23.5 0.0 copy-start.4
  23.6 6.2 %collective-permute-start.5 = (f32[4,4096]{1,0:T(4,128)S(1)}, f32[4,4096]{1,0:T(4,128)S(1)}, u32[]{:S(2)}, u32[]{:S(2)}) collective-permute-start(f32[4,4096]{1,0:T(4,128)S(1)} %collective-permute-done.4.beside), channel_id=1, source_target_pairs={{0,1},{1,0},{2,3},{3,2},{4,5},{5,4},{6,7},{7,6},{8,9},{9,8},{10,11... | collective-permute-start | bytes 196616 | tf_op jit(solution)/shard_map/ppermute | solution.py:271
  29.7 0.9 %collective-permute-done.5.relayed = f32[4,4096]{1,0:T(4,128)S(1)} collective-permute-done((f32[4,4096]{1,0:T(4,128)S(1)}, f32[4,4096]{1,0:T(4,128)S(1)}, u32[]{:S(2)}, u32[]{:S(2)}) %collective-permute-start.5) | collective-permute-done | bytes 65568 | tf_op jit(solution)/shard_map/ppermute | solution.py:271
  30.6 0.0 copy-done.4
  30.6 0.6 copy-done.7
  31.2 3.5 %shard_map.79 = (f32[8,4096]{1,0:T(8,128)}, bf16[64,4096]{1,0:T(8,128)(2,1)}, bf16[2048,128]{1,0:T(8,128)(2,1)}) custom-call(s32[1]{0:T(128)} %bitcast.slab_ref, f32[8,4096]{1,0:T(8,128)} %get-tuple-element.22.mine, f32[8,4096]{1,0:T(8,128)} %copy-done, f32[4,4096]{1,0:T(4,128)} %copy-done.4, f32[4,4096]{1,0:T(4,128)} %copy-done.7, ...), custom_call_target="tpu_custom_call" | custom-call | tf_op jit(solution)/shard_map/pallas_call | solution.py:247
  34.8 0.3 collective-permute-start.6
  35.1 1.2 %collective-permute-done.6.mate = f32[8,4096]{1,0:T(8,128)S(1)} collective-permute-done((f32[8,4096]{1,0:T(8,128)}, f32[8,4096]{1,0:T(8,128)S(1)}, u32[]{:S(2)}, u32[]{:S(2)}) %collective-permute-start.6) | collective-permute-done | bytes 131104 | tf_op jit(solution)/shard_map/ppermute | solution.py:271
  36.3 0.7 copy-done.2
  37.0 1.6 %shard_map.80 = f32[4,4096]{1,0:T(4,128)} custom-call(s32[1]{0:T(128)} %bitcast.slab_ref, f32[8,4096]{1,0:T(8,128)} %get-tuple-element.25.mine, f32[8,4096]{1,0:T(8,128)} %copy-done.2), custom_call_target="tpu_custom_call" | custom-call | tf_op jit(solution)/shard_map/pallas_call | solution.py:247
  38.6 0.7 collective-permute-start.7
  39.3 0.0 collective-permute-done.7.beside
  39.3 0.0 copy-start.6
  39.3 6.4 %collective-permute-start.8 = (f32[4,4096]{1,0:T(4,128)S(1)}, f32[4,4096]{1,0:T(4,128)S(1)}, u32[]{:S(2)}, u32[]{:S(2)}) collective-permute-start(f32[4,4096]{1,0:T(4,128)S(1)} %collective-permute-done.7.beside), channel_id=1, source_target_pairs={{0,1},{1,0},{2,3},{3,2},{4,5},{5,4},{6,7},{7,6},{8,9},{9,8},{10,11... | collective-permute-start | bytes 196616 | tf_op jit(solution)/shard_map/ppermute | solution.py:271
  45.7 0.9 %collective-permute-done.8.relayed = f32[4,4096]{1,0:T(4,128)S(1)} collective-permute-done((f32[4,4096]{1,0:T(4,128)S(1)}, f32[4,4096]{1,0:T(4,128)S(1)}, u32[]{:S(2)}, u32[]{:S(2)}) %collective-permute-start.8) | collective-permute-done | bytes 65568 | tf_op jit(solution)/shard_map/ppermute | solution.py:271
  46.6 0.0 copy-done.6
  46.6 0.6 copy-done.9
  47.2 2.7 %shard_map.81 = (f32[16,16,128]{2,1,0:T(8,128)}, f32[64,128]{1,0:T(8,128)}) custom-call(s32[1]{0:T(128)} %bitcast.slab_ref, f32[8,4096]{1,0:T(8,128)} %get-tuple-element.25.mine, f32[8,4096]{1,0:T(8,128)} %copy-done.2, f32[4,4096]{1,0:T(4,128)} %copy-done.6, f32[4,4096]{1,0:T(4,128)} %copy-done.9, bf16[64,4096]{1,0:T(8,128)(2,1)} %get-tuple-element.26.maps), custom_call_target="tpu_custom_call" | custom-call | tf_op jit(solution)/shard_map/pallas_call | solution.py:247
  49.9 14.9 %all_to_all.10.shares = f32[16,16,128]{2,1,0:T(8,128)} all-to-all(f32[16,16,128]{2,1,0:T(8,128)} %get-tuple-element.27), channel_id=1, replica_groups=mesh['vol'=2,'gz'=16] {'gz'}, dimensions={0} | all-to-all | bytes 262144 | tf_op jit(solution)/shard_map/all_to_all | solution.py:314
  64.7 2.6 %shard_map.82 = (f32[32,64]{1,0:T(8,128)}, f32[8,4096]{1,0:T(8,128)}, f32[4,4096]{1,0:T(4,128)}) custom-call(s32[1]{0:T(128)} %bitcast.slab_ref, f32[16,16,128]{2,1,0:T(8,128)} %all_to_all.10.shares, bf16[64,4096]{1,0:T(8,128)(2,1)} %get-tuple-element.26.maps), custom_call_target="tpu_custom_call" | custom-call | tf_op jit(solution)/shard_map/pallas_call | solution.py:247
  67.3 0.0 collective-permute-start.9
  67.3 0.7 collective-permute-start.10
  68.0 0.0 collective-permute-done.10.beside
  68.0 0.0 copy-start.10
  68.0 0.9 %collective-permute-done.9.mate = f32[8,4096]{1,0:T(8,128)S(1)} collective-permute-done((f32[8,4096]{1,0:T(8,128)}, f32[8,4096]{1,0:T(8,128)S(1)}, u32[]{:S(2)}, u32[]{:S(2)}) %collective-permute-start.9) | collective-permute-done | bytes 131104 | tf_op jit(solution)/shard_map/ppermute | solution.py:271
  68.9 0.6 copy-done.3
  69.5 1.7 %shard_map.83 = f32[16,128]{1,0:T(8,128)} custom-call(s32[1]{0:T(128)} %bitcast.slab_ref, f32[8,4096]{1,0:T(8,128)} %get-tuple-element.29.mine, f32[8,4096]{1,0:T(8,128)} %copy-done.3, f32[4,4096]{1,0:T(4,128)} %copy-done.10), custom_call_target="tpu_custom_call" | custom-call | tf_op jit(solution)/shard_map/pallas_call | solution.py:247
  71.2 14.6 %all_to_all.11 = f32[16,1,128]{2,1,0:T(1,128)S(1)} all-to-all(f32[16,1,128]{2,1,0:T(1,128)} %bitcast.14), channel_id=1, replica_groups=mesh['vol'=2,'gz'=16] {'gz'}, dimensions={0} | all-to-all | bytes 16384 | tf_op jit(solution)/shard_map/all_to_all | solution.py:326
  85.8 0.6 slice_reduce_fusion
  (8 shorter events, 0.0 us)
Async XLA Ops:
  3.5 1.7 %collective-permute-start = (f32[8,4096]{1,0:T(8,128)}, f32[8,4096]{1,0:T(8,128)S(1)}, u32[]{:S(2)}, u32[]{:S(2)}) collective-permute-start(f32[8,4096]{1,0:T(8,128)} %get-tuple-element.18.mine), channel_id=1, source_target_pairs={{0,1},{1,0},{2,3},{3,2},{4,5},{5,4},{6,7},{7,6},{8,9},{9,8},{10,11... | collective-permute-start | bytes 393224 | tf_op jit(solution)/shard_map/ppermute | solution.py:271
  5.2 0.6 copy-start.1
  7.5 0.7 collective-permute-start.1
  8.2 7.3 %copy-start.5 = (f32[4,4096]{1,0:T(4,128)}, f32[4,4096]{1,0:T(4,128)S(1)}, u32[]{:S(2)}) copy-start(f32[4,4096]{1,0:T(4,128)S(1)} %collective-permute-done.1.beside) | copy-start | bytes 196612
  8.2 7.3 %collective-permute-start.2 = (f32[4,4096]{1,0:T(4,128)S(1)}, f32[4,4096]{1,0:T(4,128)S(1)}, u32[]{:S(2)}, u32[]{:S(2)}) collective-permute-start(f32[4,4096]{1,0:T(4,128)S(1)} %collective-permute-done.1.beside), channel_id=1, source_target_pairs={{0,1},{1,0},{2,3},{3,2},{4,5},{5,4},{6,7},{7,6},{8,9},{9,8},{10,11... | collective-permute-start | bytes 196616 | tf_op jit(solution)/shard_map/ppermute | solution.py:271
  15.4 0.6 copy-start.8
  19.0 1.6 %collective-permute-start.3 = (f32[8,4096]{1,0:T(8,128)}, f32[8,4096]{1,0:T(8,128)S(1)}, u32[]{:S(2)}, u32[]{:S(2)}) collective-permute-start(f32[8,4096]{1,0:T(8,128)} %get-tuple-element.22.mine), channel_id=1, source_target_pairs={{0,1},{1,0},{2,3},{3,2},{4,5},{5,4},{6,7},{7,6},{8,9},{9,8},{10,11... | collective-permute-start | bytes 393224 | tf_op jit(solution)/shard_map/ppermute | solution.py:271
  20.6 0.7 copy-start
  22.9 0.7 collective-permute-start.4
  23.5 7.1 %copy-start.4 = (f32[4,4096]{1,0:T(4,128)}, f32[4,4096]{1,0:T(4,128)S(1)}, u32[]{:S(2)}) copy-start(f32[4,4096]{1,0:T(4,128)S(1)} %collective-permute-done.4.beside) | copy-start | bytes 196612
  23.6 7.1 %collective-permute-start.5 = (f32[4,4096]{1,0:T(4,128)S(1)}, f32[4,4096]{1,0:T(4,128)S(1)}, u32[]{:S(2)}, u32[]{:S(2)}) collective-permute-start(f32[4,4096]{1,0:T(4,128)S(1)} %collective-permute-done.4.beside), channel_id=1, source_target_pairs={{0,1},{1,0},{2,3},{3,2},{4,5},{5,4},{6,7},{7,6},{8,9},{9,8},{10,11... | collective-permute-start | bytes 196616 | tf_op jit(solution)/shard_map/ppermute | solution.py:271
  30.6 0.6 copy-start.7
  34.8 1.6 %collective-permute-start.6 = (f32[8,4096]{1,0:T(8,128)}, f32[8,4096]{1,0:T(8,128)S(1)}, u32[]{:S(2)}, u32[]{:S(2)}) collective-permute-start(f32[8,4096]{1,0:T(8,128)} %get-tuple-element.25.mine), channel_id=1, source_target_pairs={{0,1},{1,0},{2,3},{3,2},{4,5},{5,4},{6,7},{7,6},{8,9},{9,8},{10,11... | collective-permute-start | bytes 393224 | tf_op jit(solution)/shard_map/ppermute | solution.py:271
  36.3 0.7 copy-start.2
  38.6 0.7 collective-permute-start.7
  39.3 7.3 %copy-start.6 = (f32[4,4096]{1,0:T(4,128)}, f32[4,4096]{1,0:T(4,128)S(1)}, u32[]{:S(2)}) copy-start(f32[4,4096]{1,0:T(4,128)S(1)} %collective-permute-done.7.beside) | copy-start | bytes 196612
  39.3 7.3 %collective-permute-start.8 = (f32[4,4096]{1,0:T(4,128)S(1)}, f32[4,4096]{1,0:T(4,128)S(1)}, u32[]{:S(2)}, u32[]{:S(2)}) collective-permute-start(f32[4,4096]{1,0:T(4,128)S(1)} %collective-permute-done.7.beside), channel_id=1, source_target_pairs={{0,1},{1,0},{2,3},{3,2},{4,5},{5,4},{6,7},{7,6},{8,9},{9,8},{10,11... | collective-permute-start | bytes 196616 | tf_op jit(solution)/shard_map/ppermute | solution.py:271
  46.6 0.6 copy-start.9
  67.3 1.6 %collective-permute-start.9 = (f32[8,4096]{1,0:T(8,128)}, f32[8,4096]{1,0:T(8,128)S(1)}, u32[]{:S(2)}, u32[]{:S(2)}) collective-permute-start(f32[8,4096]{1,0:T(8,128)} %get-tuple-element.29.mine), channel_id=1, source_target_pairs={{0,1},{1,0},{2,3},{3,2},{4,5},{5,4},{6,7},{7,6},{8,9},{9,8},{10,11... | collective-permute-start | bytes 393224 | tf_op jit(solution)/shard_map/ppermute | solution.py:271
  67.3 0.7 collective-permute-start.10
  68.0 0.9 %copy-start.10 = (f32[4,4096]{1,0:T(4,128)}, f32[4,4096]{1,0:T(4,128)S(1)}, u32[]{:S(2)}) copy-start(f32[4,4096]{1,0:T(4,128)S(1)} %collective-permute-done.10.beside) | copy-start | bytes 196612
  68.9 0.6 copy-start.3
where the time goes:
time: 86.9 us; the launch traced here: 86.4 us
  blocking collectives  29.4 us (34%)
  starting transfers between devices  22.7 us (26%)
  Pallas kernels  21.2 us (24%)
  waiting for transfers between devices  7.2 us (8%)
  local copies, waits for them, and re-layouts  4.49 us (5%)
    pallas_call x9, Pallas kernels, call(): pl.pallas_call(kernel, out_shape=[jax.ShapeDtypeStruct(shape, dtype) for...  21.2 us
    ppermute x7, starting transfers between devices, to_mate(): return lax.ppermute(x, 'gz', mates)  20.1 us
    all_to_all x1, blocking collectives, per_device(): shares = lax.all_to_all(shares, 'gz', 0, 0)  14.9 us
    all_to_all x1, blocking collectives, per_device(): norms = lax.all_to_all(norms.reshape(slabs, 1, 128), 'gz', 0, 0)  14.6 us
    ppermute x7, waiting for transfers between devices, to_mate(): return lax.ppermute(x, 'gz', mates)  7.19 us
    unnamed x22, local copies, waits for them, and re-layouts  4.49 us
    ppermute x4, starting transfers between devices, to_beside(): return lax.ppermute(x, 'gz', besides)  2.61 us
  transfers between devices with their start and end apart: 11, of which 7 were waited for; matrix products, arithmetic and copies ran while one was open for 0% of the time, Pallas kernels for 0%

commit v1 on v0

--- a/solution.py
+++ b/solution.py
@@ -16,6 +16,7 @@
 F32 = jnp.float32
 BF16 = jnp.bfloat16
 CHUNK = 512
+VMEM_LIMIT = 16 << 20
 
 
 def iota(shape, dim):
@@ -250,6 +251,7 @@
         in_specs=in_specs,
         out_specs=[pl.BlockSpec(memory_space=pltpu.VMEM)] * len(outs),
         scratch_shapes=[pltpu.VMEM(shape, dtype) for shape, dtype in scratch],
+        compiler_params=pltpu.CompilerParams(vmem_limit_bytes=VMEM_LIMIT),
     )(*operands)
 
 

time: 86.9 us -> 69.1 us (0.80)
  Pallas kernels: 21.2 us -> 7.24 us
  local copies, waits for them, and re-layouts: 4.49 us -> 3.16 us
  blocking collectives: 29.4 us -> 28.3 us
    pallas_call x9, Pallas kernels: 21.2 us -> 7.24 us  [call(): pl.pallas_call(kernel, out_shape=[jax.ShapeDtypeStruct(shape, dtype) for...]
    unnamed x22 -> x8, local copies, waits for them, and re-layouts: 4.49 us -> 3.16 us
where the time goes in v1:
time: 69.1 us; the launch traced here: 68.6 us
  blocking collectives  28.3 us (41%)
  starting transfers between devices  22.2 us (32%)
  Pallas kernels  7.24 us (10%)
  waiting for transfers between devices  6.37 us (9%)
  local copies, waits for them, and re-layouts  3.16 us (5%)
  between operations  0.73 us (1%)
    ppermute x7, starting transfers between devices, to_mate(): return lax.ppermute(x, 'gz', mates)  19.6 us
    all_to_all x1, blocking collectives, per_device(): shares = lax.all_to_all(shares, 'gz', 0, 0)  14.5 us
    all_to_all x1, blocking collectives, per_device(): norms = lax.all_to_all(norms.reshape(slabs, 1, 128), 'gz', 0, 0)  13.7 us
    pallas_call x9, Pallas kernels, call(): pl.pallas_call(kernel, out_shape=[jax.ShapeDtypeStruct(shape, dtype) for...  7.24 us
    ppermute x7, waiting for transfers between devices, to_mate(): return lax.ppermute(x, 'gz', mates)  6.36 us
    unnamed x8, local copies, waits for them, and re-layouts  3.16 us
    ppermute x4, starting transfers between devices, to_beside(): return lax.ppermute(x, 'gz', besides)  2.65 us
  transfers between devices with their start and end apart: 11, of which 7 were waited for; matrix products, arithmetic and copies ran while one was open for 0% of the time, Pallas kernels for 0%

profile of v1, /device:TPU:0, one launch (start us, length us, event | category | flops | bytes accessed | tf_op | source)
XLA Modules:
  0.0 68.6 jit_solution(689371836343227210)
XLA Ops:
  0.6 0.0 copy-start
  0.6 1.0 %copy-done = bf16[32,2,32,128]{3,2,1,0:T(8,128)(2,1)S(1)} copy-done((bf16[32,2,32,128]{3,2,1,0:T(8,128)(2,1)S(1)}, bf16[32,2,32,128]{3,2,1,0:T(8,128)(2,1)}, u32[]{:S(2)}) %copy-start) | copy-done | bytes 524312
  1.7 0.0 copy-start.1
  1.7 0.8 %copy-done.1 = f32[2,32,128]{2,1,0:T(8,128)S(1)} copy-done((f32[2,32,128]{2,1,0:T(8,128)S(1)}, f32[2,32,128]{2,1,0:T(8,128)}, u32[]{:S(2)}) %copy-start.1) | copy-done | bytes 32792
  2.4 0.0 copy-start.2
  2.4 0.7 %copy-done.2 = f32[32,64]{1,0:T(8,128)S(1)} copy-done((f32[32,64]{1,0:T(8,128)S(1)}, f32[32,64]{1,0:T(8,128)}, u32[]{:S(2)}) %copy-start.2) | copy-done | bytes 8216
  3.2 1.2 %shard_map.75 = (f32[8,4096]{1,0:T(8,128)S(1)}, bf16[64,4096]{1,0:T(8,128)(2,1)S(1)}, bf16[64,128]{1,0:T(8,128)(2,1)S(1)}, bf16[128,64]{1,0:T(8,128)(2,1)S(1)}) custom-call(s32[1]{0:T(128)} %bitcast.slab_ref, bf16[2048,128]{1,0:T(8,128)(2,1)S(1)} %bitcast.10, f32[64,128]{1,0:T(8,128)S(1)} %bitcast.11, f32[32,64]{1,0:T(8,128)S(1)} %copy-done.2), custom_call_target="tpu_custom_call" | custom-call | tf_op jit(solution)/shard_map/pallas_call | solution.py:248
  4.3 0.6 collective-permute-start
  4.9 1.0 %collective-permute-done.mate = f32[8,4096]{1,0:T(8,128)S(1)} collective-permute-done((f32[8,4096]{1,0:T(8,128)S(1)}, f32[8,4096]{1,0:T(8,128)S(1)}, u32[]{:S(2)}, u32[]{:S(2)}) %collective-permute-start) | collective-permute-done | bytes 131104 | tf_op jit(solution)/shard_map/ppermute | solution.py:273
  5.9 0.7 collective-permute-start.1
  6.6 0.0 collective-permute-done.1.beside
  6.6 6.2 %collective-permute-start.2 = (f32[4,4096]{1,0:T(4,128)S(1)}, f32[4,4096]{1,0:T(4,128)S(1)}, u32[]{:S(2)}, u32[]{:S(2)}) collective-permute-start(f32[4,4096]{1,0:T(4,128)S(1)} %collective-permute-done.1.beside), channel_id=1, source_target_pairs={{0,1},{1,0},{2,3},{3,2},{4,5},{5,4},{6,7},{7,6},{8,9},{9,8},{10,11... | collective-permute-start | bytes 196616 | tf_op jit(solution)/shard_map/ppermute | solution.py:273
  12.7 0.9 %collective-permute-done.2.relayed = f32[4,4096]{1,0:T(4,128)S(1)} collective-permute-done((f32[4,4096]{1,0:T(4,128)S(1)}, f32[4,4096]{1,0:T(4,128)S(1)}, u32[]{:S(2)}, u32[]{:S(2)}) %collective-permute-start.2) | collective-permute-done | bytes 65568 | tf_op jit(solution)/shard_map/ppermute | solution.py:273
  13.6 0.0 copy-start.3
  13.6 0.7 copy-done.3
  14.3 1.1 %shard_map.77 = (f32[8,4096]{1,0:T(8,128)S(1)}, bf16[64,4096]{1,0:T(8,128)(2,1)S(1)}) custom-call(s32[1]{0:T(128)} %bitcast.slab_ref, f32[8,4096]{1,0:T(8,128)S(1)} %get-tuple-element.18.mine, f32[8,4096]{1,0:T(8,128)S(1)} %collective-permute-done.mate, f32[4,4096]{1,0:T(4,128)S(1)} %collective-permute-done.1.beside, ...), custom_call_target="tpu_custom_call" | custom-call | tf_op jit(solution)/shard_map/pallas_call | solution.py:248
  15.4 0.4 collective-permute-start.3
  15.8 1.0 %collective-permute-done.3.mate = f32[8,4096]{1,0:T(8,128)S(1)} collective-permute-done((f32[8,4096]{1,0:T(8,128)S(1)}, f32[8,4096]{1,0:T(8,128)S(1)}, u32[]{:S(2)}, u32[]{:S(2)}) %collective-permute-start.3) | collective-permute-done | bytes 131104 | tf_op jit(solution)/shard_map/ppermute | solution.py:273
  16.8 0.7 collective-permute-start.4
  17.5 0.0 collective-permute-done.4.beside
  17.5 5.9 %collective-permute-start.5 = (f32[4,4096]{1,0:T(4,128)S(1)}, f32[4,4096]{1,0:T(4,128)S(1)}, u32[]{:S(2)}, u32[]{:S(2)}) collective-permute-start(f32[4,4096]{1,0:T(4,128)S(1)} %collective-permute-done.4.beside), channel_id=1, source_target_pairs={{0,1},{1,0},{2,3},{3,2},{4,5},{5,4},{6,7},{7,6},{8,9},{9,8},{10,11... | collective-permute-start | bytes 196616 | tf_op jit(solution)/shard_map/ppermute | solution.py:273
  23.4 0.9 %collective-permute-done.5.relayed = f32[4,4096]{1,0:T(4,128)S(1)} collective-permute-done((f32[4,4096]{1,0:T(4,128)S(1)}, f32[4,4096]{1,0:T(4,128)S(1)}, u32[]{:S(2)}, u32[]{:S(2)}) %collective-permute-start.5) | collective-permute-done | bytes 65568 | tf_op jit(solution)/shard_map/ppermute | solution.py:273
  24.3 2.3 %shard_map.79 = (f32[8,4096]{1,0:T(8,128)S(1)}, bf16[64,4096]{1,0:T(8,128)(2,1)S(1)}, bf16[2048,128]{1,0:T(8,128)(2,1)}) custom-call(s32[1]{0:T(128)} %bitcast.slab_ref, f32[8,4096]{1,0:T(8,128)S(1)} %get-tuple-element.22.mine, f32[8,4096]{1,0:T(8,128)S(1)} %collective-permute-done.3.mate, f32[4,4096]{1,0:T(4,128)S(1)} %collective-permute-done.4.beside, ...), custom_call_target="tpu_custom_call" | custom-call | tf_op jit(solution)/shard_map/pallas_call | solution.py:248
  26.6 0.4 collective-permute-start.6
  27.0 1.0 %collective-permute-done.6.mate = f32[8,4096]{1,0:T(8,128)S(1)} collective-permute-done((f32[8,4096]{1,0:T(8,128)S(1)}, f32[8,4096]{1,0:T(8,128)S(1)}, u32[]{:S(2)}, u32[]{:S(2)}) %collective-permute-start.6) | collective-permute-done | bytes 131104 | tf_op jit(solution)/shard_map/ppermute | solution.py:273
  28.0 0.7 collective-permute-start.7
  28.7 0.0 collective-permute-done.7.beside
  28.7 6.2 %collective-permute-start.8 = (f32[4,4096]{1,0:T(4,128)S(1)}, f32[4,4096]{1,0:T(4,128)S(1)}, u32[]{:S(2)}, u32[]{:S(2)}) collective-permute-start(f32[4,4096]{1,0:T(4,128)S(1)} %collective-permute-done.7.beside), channel_id=1, source_target_pairs={{0,1},{1,0},{2,3},{3,2},{4,5},{5,4},{6,7},{7,6},{8,9},{9,8},{10,11... | collective-permute-start | bytes 196616 | tf_op jit(solution)/shard_map/ppermute | solution.py:273
  34.8 0.9 %collective-permute-done.8.relayed = f32[4,4096]{1,0:T(4,128)S(1)} collective-permute-done((f32[4,4096]{1,0:T(4,128)S(1)}, f32[4,4096]{1,0:T(4,128)S(1)}, u32[]{:S(2)}, u32[]{:S(2)}) %collective-permute-start.8) | collective-permute-done | bytes 65568 | tf_op jit(solution)/shard_map/ppermute | solution.py:273
  35.8 1.2 %shard_map.81 = (f32[16,16,128]{2,1,0:T(8,128)S(1)}, f32[64,128]{1,0:T(8,128)}) custom-call(s32[1]{0:T(128)} %bitcast.slab_ref, f32[8,4096]{1,0:T(8,128)S(1)} %get-tuple-element.25.mine, f32[8,4096]{1,0:T(8,128)S(1)} %collective-permute-done.6.mate, f32[4,4096]{1,0:T(4,128)S(1)} %collective-permute-done.7.beside, ...), custom_call_target="tpu_custom_call" | custom-call | tf_op jit(solution)/shard_map/pallas_call | solution.py:248
  37.0 14.5 %all_to_all.10.shares = f32[16,16,128]{2,1,0:T(8,128)S(1)} all-to-all(f32[16,16,128]{2,1,0:T(8,128)S(1)} %get-tuple-element.27), channel_id=1, replica_groups=mesh['vol'=2,'gz'=16] {'gz'}, dimensions={0} | all-to-all | bytes 262144 | tf_op jit(solution)/shard_map/all_to_all | solution.py:316
  51.5 1.3 %shard_map.82 = (f32[32,64]{1,0:T(8,128)}, f32[8,4096]{1,0:T(8,128)S(1)}, f32[4,4096]{1,0:T(4,128)S(1)}) custom-call(s32[1]{0:T(128)} %bitcast.slab_ref, f32[16,16,128]{2,1,0:T(8,128)S(1)} %all_to_all.10.shares, bf16[64,4096]{1,0:T(8,128)(2,1)S(1)} %get-tuple-element.26.maps), custom_call_target="tpu_custom_call" | custom-call | tf_op jit(solution)/shard_map/pallas_call | solution.py:248
  52.8 0.0 collective-permute-start.9
  52.8 0.7 collective-permute-start.10
  53.5 0.0 collective-permute-done.10.beside
  53.5 0.7 collective-permute-done.9.mate
  54.1 0.1 shard_map.83
  54.3 13.7 %all_to_all.11 = f32[16,1,128]{2,1,0:T(1,128)S(1)} all-to-all(f32[16,1,128]{2,1,0:T(1,128)S(1)} %bitcast.14), channel_id=1, replica_groups=mesh['vol'=2,'gz'=16] {'gz'}, dimensions={0} | all-to-all | bytes 16384 | tf_op jit(solution)/shard_map/all_to_all | solution.py:328
  68.0 0.6 slice_reduce_fusion
  (3 shorter events, 0.1 us)
Async XLA Ops:
  0.6 1.0 %copy-start = (bf16[32,2,32,128]{3,2,1,0:T(8,128)(2,1)S(1)}, bf16[32,2,32,128]{3,2,1,0:T(8,128)(2,1)}, u32[]{:S(2)}) copy-start(bf16[32,2,32,128]{3,2,1,0:T(8,128)(2,1)} %param.5) | copy-start | bytes 1572868
  1.7 0.8 %copy-start.1 = (f32[2,32,128]{2,1,0:T(8,128)S(1)}, f32[2,32,128]{2,1,0:T(8,128)}, u32[]{:S(2)}) copy-start(f32[2,32,128]{2,1,0:T(8,128)} %param.4) | copy-start | bytes 98308
  2.4 0.7 %copy-start.2 = (f32[32,64]{1,0:T(8,128)S(1)}, f32[32,64]{1,0:T(8,128)}, u32[]{:S(2)}) copy-start(f32[32,64]{1,0:T(8,128)} %atoms.1) | copy-start | bytes 24580
  4.3 1.5 %collective-permute-start = (f32[8,4096]{1,0:T(8,128)S(1)}, f32[8,4096]{1,0:T(8,128)S(1)}, u32[]{:S(2)}, u32[]{:S(2)}) collective-permute-start(f32[8,4096]{1,0:T(8,128)S(1)} %get-tuple-element.18.mine), channel_id=1, source_target_pairs={{0,1},{1,0},{2,3},{3,2},{4,5},{5,4},{6,7},{7,6},{8,9},{9,8},{10,11... | collective-permute-start | bytes 393224 | tf_op jit(solution)/shard_map/ppermute | solution.py:273
  5.9 0.7 collective-permute-start.1
  6.6 7.1 %collective-permute-start.2 = (f32[4,4096]{1,0:T(4,128)S(1)}, f32[4,4096]{1,0:T(4,128)S(1)}, u32[]{:S(2)}, u32[]{:S(2)}) collective-permute-start(f32[4,4096]{1,0:T(4,128)S(1)} %collective-permute-done.1.beside), channel_id=1, source_target_pairs={{0,1},{1,0},{2,3},{3,2},{4,5},{5,4},{6,7},{7,6},{8,9},{9,8},{10,11... | collective-permute-start | bytes 196616 | tf_op jit(solution)/shard_map/ppermute | solution.py:273
  13.6 0.7 copy-start.3
  15.4 1.4 %collective-permute-start.3 = (f32[8,4096]{1,0:T(8,128)S(1)}, f32[8,4096]{1,0:T(8,128)S(1)}, u32[]{:S(2)}, u32[]{:S(2)}) collective-permute-start(f32[8,4096]{1,0:T(8,128)S(1)} %get-tuple-element.22.mine), channel_id=1, source_target_pairs={{0,1},{1,0},{2,3},{3,2},{4,5},{5,4},{6,7},{7,6},{8,9},{9,8},{10,11... | collective-permute-start | bytes 393224 | tf_op jit(solution)/shard_map/ppermute | solution.py:273
  16.8 0.7 collective-permute-start.4
  17.5 6.9 %collective-permute-start.5 = (f32[4,4096]{1,0:T(4,128)S(1)}, f32[4,4096]{1,0:T(4,128)S(1)}, u32[]{:S(2)}, u32[]{:S(2)}) collective-permute-start(f32[4,4096]{1,0:T(4,128)S(1)} %collective-permute-done.4.beside), channel_id=1, source_target_pairs={{0,1},{1,0},{2,3},{3,2},{4,5},{5,4},{6,7},{7,6},{8,9},{9,8},{10,11... | collective-permute-start | bytes 196616 | tf_op jit(solution)/shard_map/ppermute | solution.py:273
  26.6 1.3 %collective-permute-start.6 = (f32[8,4096]{1,0:T(8,128)S(1)}, f32[8,4096]{1,0:T(8,128)S(1)}, u32[]{:S(2)}, u32[]{:S(2)}) collective-permute-start(f32[8,4096]{1,0:T(8,128)S(1)} %get-tuple-element.25.mine), channel_id=1, source_target_pairs={{0,1},{1,0},{2,3},{3,2},{4,5},{5,4},{6,7},{7,6},{8,9},{9,8},{10,11... | collective-permute-start | bytes 393224 | tf_op jit(solution)/shard_map/ppermute | solution.py:273
  28.0 0.7 collective-permute-start.7
  28.7 7.1 %collective-permute-start.8 = (f32[4,4096]{1,0:T(4,128)S(1)}, f32[4,4096]{1,0:T(4,128)S(1)}, u32[]{:S(2)}, u32[]{:S(2)}) collective-permute-start(f32[4,4096]{1,0:T(4,128)S(1)} %collective-permute-done.7.beside), channel_id=1, source_target_pairs={{0,1},{1,0},{2,3},{3,2},{4,5},{5,4},{6,7},{7,6},{8,9},{9,8},{10,11... | collective-permute-start | bytes 196616 | tf_op jit(solution)/shard_map/ppermute | solution.py:273
  52.8 1.3 %collective-permute-start.9 = (f32[8,4096]{1,0:T(8,128)S(1)}, f32[8,4096]{1,0:T(8,128)S(1)}, u32[]{:S(2)}, u32[]{:S(2)}) collective-permute-start(f32[8,4096]{1,0:T(8,128)S(1)} %get-tuple-element.29.mine), channel_id=1, source_target_pairs={{0,1},{1,0},{2,3},{3,2},{4,5},{5,4},{6,7},{7,6},{8,9},{9,8},{10,11... | collective-permute-start | bytes 393224 | tf_op jit(solution)/shard_map/ppermute | solution.py:273
  52.8 0.7 collective-permute-start.10

commit v2 on v1

v2 whole, which is shorter than its diff:
```python
import functools
import math

import jax
import jax.numpy as jnp
from jax import lax
from jax.experimental import pallas as pl
from jax.experimental.pallas import tpu as pltpu
from jax.sharding import PartitionSpec as P

coef_step = 0.015
second_t = (1.0 + math.sqrt(5.0)) / 2.0
third_t = (1.0 + math.sqrt(1.0 + 4.0 * second_t * second_t)) / 2.0
momentum = (second_t - 1.0) / third_t

F32 = jnp.float32
BF16 = jnp.bfloat16
CHUNK = 512
VMEM_LIMIT = 16 << 20


def iota(shape, dim):
    return lax.broadcasted_iota(jnp.int32, shape, dim)


def tap_select(slab, plane, shape, tap_dim):
    tap, col = iota(shape, tap_dim), iota(shape, 1 - tap_dim)
    lands = (2 * slab + plane - 1 + (tap >> 4)) & 7
    return (((tap & 15) == (col >> 3)) & (lands == (col & 7))).astype(BF16)


def taps_dot(lhs, rhs, dims):
    return lax.dot_general(lhs, rhs, (dims, ((), ())), preferred_element_type=F32)


def bank_rows(atoms, slab):
    parts = [taps_dot(atoms, tap_select(slab, z, (64, 128), 0), ((1,), (0,))) for z in range(2)]
    return jnp.concatenate(parts, axis=0).astype(BF16)


def bank_cols(atoms, slab):
    parts = [taps_dot(tap_select(slab, z, (128, 64), 1), atoms, ((1,), (1,))) for z in range(2)]
    return jnp.concatenate(parts, axis=1).astype(BF16)


def spread(pairs, products, height, breadth, emit):
    zeros = jnp.zeros((128, 2 * breadth), F32)
    size = height * breadth
    products[:, : 2 * breadth] = zeros
    products[:, 2 * breadth + size :] = zeros[:, :breadth]
    for start in range(0, size, CHUNK):
        part = slice(start, start + CHUNK)
        terms = [jnp.dot(bank, maps[:, part], preferred_element_type=F32) for bank, maps in pairs]
        products[:, 2 * breadth + start : 2 * breadth + start + CHUNK] = sum(terms[1:], terms[0])
    lane = iota((8, breadth), 1)
    for y in range(height):
        sums = []
        for col in range(4):
            terms = [
                products[
                    (4 * row + col) * 8 : (4 * row + col) * 8 + 8,
                    (y + 3 - row) * breadth : (y + 4 - row) * breadth,
                ]
                for row in range(4)
            ]
            sums.append((terms[0] + terms[1]) + (terms[2] + terms[3]))
        total = sums[1] + jnp.where(lane < breadth - 1, pltpu.roll(sums[0], breadth - 1, 1), 0.0)
        total += jnp.where(lane >= 1, pltpu.roll(sums[2], 1, 1), 0.0)
        total += jnp.where(lane >= 2, pltpu.roll(sums[3], 2, 1), 0.0)
        emit(y, total)


def emit_share(slab, tomo, share, height, breadth):
    row = iota((8, breadth), 0)
    first, second = row == ((2 * slab) & 7), row == ((2 * slab + 1) & 7)

    def emit(y, total):
        own = jnp.where(first, tomo[y : y + 1, :], jnp.where(second, tomo[height + y : height + y + 1, :], 0.0))
        share[:, y * breadth : (y + 1) * breadth] = own - total

    return emit


def plane_offset(slab, shape):
    return (iota(shape, 0) - (2 * slab - 1)) & 7


def sent_range(slab, offset):
    low = 2 * (slab & 1)
    return (offset >= low) & (offset <= low + 2)


def gather_resid(slab, slabs, mine, mate, beside, relayed, height, breadth, visit):
    offset = plane_offset(slab, (8, breadth))
    from_beside = sent_range(slab, offset)
    from_relay = offset == 4 * (1 - (slab & 1))
    plane = 2 * slab - 1 + offset
    valid = (offset < 5) & (plane >= 0) & (plane < 2 * slabs)
    if relayed is None:
        valid &= ~from_relay
    for y in range(height):
        cols = slice(y * breadth, (y + 1) * breadth)
        near = beside[:, cols]
        total = mine[:, cols] + mate[:, cols]
        total += jnp.where(from_beside, jnp.concatenate([near, near], axis=0), 0.0)
        if relayed is not None:
            far = relayed[:, cols]
            total += jnp.where(from_relay, jnp.concatenate([far, far], axis=0), 0.0)
        visit(y, jnp.where(valid, total, 0.0))


def unfold(resid, unfolded, height, breadth, y):
    lane = iota((8, breadth), 1)
    shifted = [
        jnp.where(lane >= 1, pltpu.roll(resid, 1, 1), 0.0),
        resid,
        jnp.where(lane < breadth - 1, pltpu.roll(resid, breadth - 1, 1), 0.0),
        jnp.where(lane < breadth - 2, pltpu.roll(resid, breadth - 2, 1), 0.0),
    ]
    halves = [jnp.concatenate(shifted[k : k + 2], axis=0).astype(BF16) for k in (0, 2)]
    for row in range(4):
        target = y - row + 1
        if 0 <= target < height:
            for k in range(2):
                start = row * 32 + k * 16
                unfolded[start : start + 16, target * breadth : (target + 1) * breadth] = halves[k]


def unfold_edges(unfolded, height, breadth):
    zeros = jnp.zeros((32, breadth), BF16)
    for row in range(4):
        for y in range(height):
            if not 0 <= y + row - 1 < height:
                unfolded[row * 32 : row * 32 + 32, y * breadth : (y + 1) * breadth] = zeros


def start_kernel(
    height, breadth, slab_ref, maps, tomo, atoms, limits,
    share, by_voxel, rows_out, cols_out, tomo_out, limits_out,
    natural, bank_in, limits_in, wide, products, sems,
):
    slab = slab_ref[0]
    atom_count = by_voxel.shape[0] // 2
    half = maps.shape[0] // 2
    copies = [
        pltpu.make_async_copy(atoms, bank_in, sems.at[0]),
        pltpu.make_async_copy(maps.at[:half], natural.at[:half], sems.at[1]),
        pltpu.make_async_copy(maps.at[half:], natural.at[half:], sems.at[2]),
        pltpu.make_async_copy(tomo, tomo_out, sems.at[3]),
        pltpu.make_async_copy(limits, limits_in, sems.at[4]),
    ]
    for copy in copies:
        copy.start()
    copies[0].wait()
    bank = bank_in[...].astype(BF16)
    rows_out[...] = bank_rows(bank, slab)
    cols = bank_cols(bank, slab)
    cols_out[...] = cols
    group = atom_count // 2
    for part in range(2):
        copies[1 + part].wait()
        span = slice(part * half, (part + 1) * half)
        wide[span, :] = natural[span, :].astype(F32)
        for y in range(height):
            for z in range(2):
                rows = wide[pl.ds(part * half + z * height + y, group, stride=2 * height), :]
                first = z * atom_count + part * group
                by_voxel[first : first + group, y * breadth : (y + 1) * breadth] = rows.astype(BF16)
    copies[3].wait()
    copies[4].wait()
    square = (atom_count, atom_count)
    column = jnp.sum(jnp.where(iota(square, 0) == iota(square, 1), limits_in[...], 0.0), axis=1, keepdims=True)
    limits_out[...] = jnp.broadcast_to(jnp.concatenate([column, column], axis=0), limits_out.shape)
    spread([(cols, by_voxel)], products, height, breadth, emit_share(slab, tomo_out, share, height, breadth))


def relay_kernel(slab_ref, mine, mate, out):
    slab = slab_ref[0]
    total = mine[...] + mate[...]
    total = jnp.where(sent_range(slab, plane_offset(slab, total.shape)), total, 0.0)
    out[...] = total[:4] + total[4:]


def step_kernel(
    height, breadth, slabs, last, slab_ref, mine, mate, beside, relayed, maps, tomo, rows, cols, limits,
    share, by_voxel, unfolded, products,
):
    slab = slab_ref[0]
    size = height * breadth
    unfold_edges(unfolded, height, breadth)
    gather_resid(
        slab, slabs, mine, mate, beside, relayed, height, breadth,
        lambda y, resid: unfold(resid, unfolded, height, breadth, y),
    )
    limit = jnp.concatenate([limits[...]] * (CHUNK // limits.shape[1]), axis=1)
    bank = rows[...]
    for start in range(0, size, CHUNK):
        part = slice(start, start + CHUNK)
        gradient = jnp.dot(bank, unfolded[:, part], preferred_element_type=F32)
        before = maps[:, part].astype(F32)
        moved = before - coef_step * gradient
        after = (moved - jnp.clip(moved, -limit, limit)).astype(BF16)
        if not last:
            after = after.astype(F32)
            after = (after + momentum * (after - before)).astype(BF16)
        by_voxel[:, part] = after
    spread([(cols[...], by_voxel)], products, height, breadth, emit_share(slab, tomo, share, height, breadth))


def natural_kernel(height, breadth, maps, natural, wide):
    atom_count = maps.shape[0] // 2
    for y in range(height):
        rows = maps[:, y * breadth : (y + 1) * breadth].astype(F32)
        for z in range(2):
            wide[pl.ds(z * height + y, atom_count, stride=2 * height), :] = rows[z * atom_count : (z + 1) * atom_count]
    natural[...] = wide[...].astype(BF16)


def descent_kernel(
    height, breadth, slabs, slab_ref, mine, mate, beside, maps, mate_maps, shares, resid_out, unfolded, planes
):
    slab = slab_ref[0]
    odd = slab & 1
    atom_count = maps.shape[0] // 2
    unfold_edges(unfolded, height, breadth)

    def visit(y, resid):
        planes[8 * y : 8 * y + 8, :] = resid
        unfold(resid, unfolded, height, breadth, y)

    gather_resid(slab, slabs, mine, mate, beside, None, height, breadth, visit)
    for z in range(2):
        resid_out[z * height : (z + 1) * height, :] = planes[pl.ds((2 * slab + z) & 7, height, stride=8), :]
    start = pl.multiple_of(odd * atom_count, atom_count)
    terms = [
        (taps_dot(maps[...], unfolded[...], ((1,), (1,))), 0, False),
        (taps_dot(mate_maps[pl.ds(start, atom_count), :], unfolded[...], ((1,), (1,))), 2 - 3 * odd, True),
    ]
    tap = iota((128, 64), 1) >> 4
    total = jnp.zeros((atom_count, 64), F32)
    for both, plane, edge in terms:
        for z in range(both.shape[0] // atom_count):
            left = both[z * atom_count : (z + 1) * atom_count, :]
            pick = tap_select(slab, plane + z, (128, 64), 1)
            if edge:
                pick = jnp.where(tap == 3 * odd, pick, jnp.zeros_like(pick))
            for _ in range(3):
                head = left.astype(BF16)
                total += taps_dot(head, pick, ((1,), (0,)))
                left = left - head.astype(F32)
    half = atom_count // 2
    packed = jnp.concatenate([total[:half], total[half:]], axis=1)
    for j in range(slabs):
        shares[j] = packed


def probe_kernel(height, breadth, slab_ref, shares, maps, mate_maps, beside_maps, descent_out, norms, products, folded):
    slab = slab_ref[0]
    packed = jnp.sum(shares[...], axis=0)
    descent = jnp.concatenate([packed[:, :64], packed[:, 64:]], axis=0)
    descent_out[...] = descent
    half = descent.astype(BF16)
    row = iota((8, breadth), 0)
    own = (row == ((2 * slab) & 7)) | (row == ((2 * slab + 1) & 7))
    odd = slab & 1
    folded[...] = jnp.zeros_like(folded)

    def emit(y, total):
        folded[...] += jnp.where(own, total * total, 0.0)

    pairs = [
        (bank_cols(half, slab), maps),
        (bank_cols(half, slab + 1 - 2 * odd), mate_maps),
        (bank_cols(half, slab - 1 + 2 * odd), beside_maps),
    ]
    spread(pairs, products, height, breadth, emit)
    total = jnp.sum(jnp.sum(folded[...], axis=1, keepdims=True), axis=0, keepdims=True)
    norms[...] = jnp.broadcast_to(total, norms.shape)


def call(kernel, outs, operands, scratch=(), spaces=None):
    spaces = spaces or [pltpu.SMEM] + [pltpu.VMEM] * (len(operands) - 1)
    return pl.pallas_call(
        kernel,
        out_shape=[jax.ShapeDtypeStruct(shape, dtype) for shape, dtype in outs],
        in_specs=[pl.BlockSpec(memory_space=space) for space in spaces],
        out_specs=[pl.BlockSpec(memory_space=pltpu.VMEM)] * len(outs),
        scratch_shapes=[pltpu.VMEM(*item) if isinstance(item, tuple) else item for item in scratch],
        compiler_params=pltpu.CompilerParams(vmem_limit_bytes=VMEM_LIMIT),
    )(*operands)


def per_device(tomogram, initial_maps, dictionary, thresholds):
    slabs = lax.axis_size("gz")
    planes, height, breadth = tomogram.shape
    atom_count = initial_maps.shape[0]
    size = height * breadth
    slab = lax.axis_index("gz").astype(jnp.int32).reshape(1)
    tomo = tomogram.reshape(planes * height, breadth)
    natural = initial_maps.reshape(atom_count * planes * height, breadth)
    limits = thresholds.reshape(1, atom_count)
    natural, tomo, dictionary, limits = (
        pltpu.with_memory_space_constraint(x, pltpu.HBM) for x in (natural, tomo, dictionary, limits)
    )

    mates = [(i, i ^ 1) for i in range(slabs)]
    besides = [(i, i + 1) for i in range(1, slabs - 1, 2)]
    besides += [(j, i) for i, j in besides]

    def to_mate(x):
        return lax.ppermute(x, "gz", mates)

    def to_beside(x):
        return lax.ppermute(x, "gz", besides)

    share_shape = ((8, size), F32)
    maps_shape = ((2 * atom_count, size), BF16)
    natural_shape = (natural.shape, BF16)
    products = ((128, size + 3 * breadth), F32)
    unfolded = ((128, size), BF16)
    wide = (natural.shape, F32)

    def meet(mine):
        mate = to_mate(mine)
        (send,) = call(relay_kernel, [((4, size), F32)], (slab, mine, mate))
        return mine, mate, send

    def step(share, maps, last):
        mine, mate, send = meet(share)
        beside = to_beside(send)
        return call(
            functools.partial(step_kernel, height, breadth, slabs, last),
            [share_shape, maps_shape],
            (slab, mine, mate, beside, to_mate(beside), maps, tomo, rows, cols, limits),
            [unfolded, products],
        )

    share, maps, rows, cols, tomo, limits = call(
        functools.partial(start_kernel, height, breadth),
        [
            share_shape,
            maps_shape,
            ((2 * atom_count, 128), BF16),
            ((128, 2 * atom_count), BF16),
            (tomo.shape, F32),
            ((2 * atom_count, 128), F32),
        ],
        (slab, natural, tomo, dictionary, limits),
        [
            natural_shape,
            (dictionary.shape, F32),
            (limits.shape, F32),
            wide,
            products,
            pltpu.SemaphoreType.DMA((5,)),
        ],
        [pltpu.SMEM] + [pltpu.HBM] * 4,
    )
    share, maps = step(share, maps, False)
    share, maps = step(share, maps, True)
    mine, mate, send = meet(share)
    send, maps = lax.optimization_barrier((send, maps))
    beside = to_beside(send)
    mate_maps = to_mate(maps)
    beside_maps = to_beside(maps)
    (natural,) = call(
        functools.partial(natural_kernel, height, breadth), [natural_shape], (maps,), [wide], [pltpu.VMEM]
    )
    shares, residual = call(
        functools.partial(descent_kernel, height, breadth, slabs),
        [((slabs, atom_count // 2, 128), F32), (tomo.shape, F32)],
        (slab, mine, mate, beside, maps, mate_maps),
        [unfolded, ((8 * height, breadth), F32)],
    )
    shares = lax.all_to_all(shares, "gz", 0, 0)
    descent, norms = call(
        functools.partial(probe_kernel, height, breadth),
        [((atom_count, 64), F32), ((slabs, 128), F32)],
        (slab, shares, maps, mate_maps, beside_maps),
        [products, ((8, breadth), F32)],
    )
    norms = lax.all_to_all(norms.reshape(slabs, 1, 128), "gz", 0, 0)
    curvature = jnp.sum(norms[:, :, :1]).reshape(1)
    return (
        natural.reshape(initial_maps.shape),
        descent,
        curvature,
        residual.reshape(tomogram.shape),
    )


def solution(mesh):
    return jax.shard_map(
        per_device,
        mesh=mesh,
        in_specs=(P(("vol", "gz"), None, None), P(None, ("vol", "gz"), None, None), P(), P()),
        out_specs=(
            P(None, ("vol", "gz"), None, None),
            P("vol", None),
            P("vol"),
            P(("vol", "gz"), None, None),
        ),
        check_vma=False,
    )
```

time: 69.1 us -> 71.4 us (1.033)
  blocking collectives: 28.3 us -> 0 us
  starting transfers between devices: 22.2 us -> 42.5 us
  waiting for transfers between devices: 6.37 us -> 17.4 us
  local copies, waits for them, and re-layouts: 3.16 us -> 0 us
  Pallas kernels: 7.24 us -> 9.76 us
    all_to_all x2 -> x0, blocking collectives: 28.3 us -> none  [the longest x1 14.5 us: per_device(): shares = lax.all_to_all(shares, 'gz', 0, 0)]
    all_to_all x0 -> x2, starting transfers between devices: none -> 25.9 us  [the longest x1 22.5 us: per_device(): shares = lax.all_to_all(shares, 'gz', 0, 0)]
    all_to_all x0 -> x2, waiting for transfers between devices: none -> 12.4 us  [the longest x1 7.89 us: per_device(): shares = lax.all_to_all(shares, 'gz', 0, 0)]
    ppermute x7 -> x6, starting transfers between devices: 19.6 us -> 13.9 us  [to_mate(): return lax.ppermute(x, 'gz', mates)]
    unnamed x8 -> x0, local copies, waits for them, and re-layouts: 3.16 us -> none
    pallas_call x9, Pallas kernels: 7.24 us -> 9.76 us  [call(): pl.pallas_call(kernel, out_shape=[jax.ShapeDtypeStruct(shape, dtype) for...]
    ppermute x7 -> x6, waiting for transfers between devices: 6.36 us -> 4.96 us  [to_mate(): return lax.ppermute(x, 'gz', mates)]
  transfers between devices with their start and end apart: 11 -> 12, of which waited for: 7 -> 8; matrix products, arithmetic and copies ran while one was open for 0% -> 0% of each run, Pallas kernels for 0% -> 5%
where the time goes in v2:
time: 71.4 us; the launch traced here: 71 us
  starting transfers between devices  42.5 us (60%)
  waiting for transfers between devices  17.4 us (24%)
  Pallas kernels  9.76 us (14%)
  between operations  0.75 us (1%)
    all_to_all x1, starting transfers between devices, per_device(): shares = lax.all_to_all(shares, 'gz', 0, 0)  22.5 us
    ppermute x6, starting transfers between devices, to_mate(): return lax.ppermute(x, 'gz', mates)  13.9 us
    pallas_call x9, Pallas kernels, call(): pl.pallas_call(kernel, out_shape=[jax.ShapeDtypeStruct(shape, dtype) for...  9.76 us
    all_to_all x1, waiting for transfers between devices, per_device(): shares = lax.all_to_all(shares, 'gz', 0, 0)  7.89 us
    ppermute x6, waiting for transfers between devices, to_mate(): return lax.ppermute(x, 'gz', mates)  4.96 us
    all_to_all x1, waiting for transfers between devices, per_device(): norms = lax.all_to_all(norms.reshape(slabs, 1, 128), 'gz', 0, 0)  4.51 us
    all_to_all x1, starting transfers between devices, per_device(): norms = lax.all_to_all(norms.reshape(slabs, 1, 128), 'gz', 0, 0)  3.43 us
    ppermute x4, starting transfers between devices, to_beside(): return lax.ppermute(x, 'gz', besides)  2.68 us
  transfers between devices with their start and end apart: 12, of which 8 were waited for; matrix products, arithmetic and copies ran while one was open for 0% of the time, Pallas kernels for 5%

profile of v2, /device:TPU:0, one launch (start us, length us, event | category | flops | bytes accessed | tf_op | source)
XLA Modules:
  0.0 71.0 jit_solution(16778833917382254510)
XLA Ops:
  0.6 2.2 %shard_map.75 = (f32[8,4096]{1,0:T(8,128)S(1)}, bf16[64,4096]{1,0:T(8,128)(2,1)S(1)}, bf16[64,128]{1,0:T(8,128)(2,1)S(1)}, bf16[128,64]{1,0:T(8,128)(2,1)S(1)}, ...) custom-call(s32[1]{0:T(128)} %bitcast.slab_ref, bf16[2048,128]{1,0:T(8,128)(2,1)} %bitcast.10, f32[64,128]{1,0:T(8,128)} %bitcast.12, ...), custom_call_target="tpu_custom_call" | custom-call | tf_op jit(solution)/shard_map/pallas_call | solution.py:283
  2.8 0.6 collective-permute-start
  3.4 1.0 %collective-permute-done.mate = f32[8,4096]{1,0:T(8,128)S(1)} collective-permute-done((f32[8,4096]{1,0:T(8,128)S(1)}, f32[8,4096]{1,0:T(8,128)S(1)}, u32[]{:S(2)}, u32[]{:S(2)}) %collective-permute-start) | collective-permute-done | bytes 131104 | tf_op jit(solution)/shard_map/ppermute | solution.py:311
  4.4 0.7 collective-permute-start.1
  5.1 0.0 collective-permute-done.1.beside
  5.1 6.2 %collective-permute-start.2 = (f32[4,4096]{1,0:T(4,128)S(1)}, f32[4,4096]{1,0:T(4,128)S(1)}, u32[]{:S(2)}, u32[]{:S(2)}) collective-permute-start(f32[4,4096]{1,0:T(4,128)S(1)} %collective-permute-done.1.beside), channel_id=1, source_target_pairs={{0,1},{1,0},{2,3},{3,2},{4,5},{5,4},{6,7},{7,6},{8,9},{9,8},{10,11... | collective-permute-start | bytes 196616 | tf_op jit(solution)/shard_map/ppermute | solution.py:311
  11.3 0.9 %collective-permute-done.2.relayed = f32[4,4096]{1,0:T(4,128)S(1)} collective-permute-done((f32[4,4096]{1,0:T(4,128)S(1)}, f32[4,4096]{1,0:T(4,128)S(1)}, u32[]{:S(2)}, u32[]{:S(2)}) %collective-permute-start.2) | collective-permute-done | bytes 65568 | tf_op jit(solution)/shard_map/ppermute | solution.py:311
  12.2 1.0 %shard_map.77 = (f32[8,4096]{1,0:T(8,128)S(1)}, bf16[64,4096]{1,0:T(8,128)(2,1)S(1)}) custom-call(s32[1]{0:T(128)} %bitcast.slab_ref, f32[8,4096]{1,0:T(8,128)S(1)} %get-tuple-element.20.mine, f32[8,4096]{1,0:T(8,128)S(1)} %collective-permute-done.mate, f32[4,4096]{1,0:T(4,128)S(1)} %collective-permute-done.1.beside, ...), custom_call_target="tpu_custom_call" | custom-call | tf_op jit(solution)/shard_map/pallas_call | solution.py:283
  13.2 0.4 collective-permute-start.3
  13.6 1.0 %collective-permute-done.3.mate = f32[8,4096]{1,0:T(8,128)S(1)} collective-permute-done((f32[8,4096]{1,0:T(8,128)S(1)}, f32[8,4096]{1,0:T(8,128)S(1)}, u32[]{:S(2)}, u32[]{:S(2)}) %collective-permute-start.3) | collective-permute-done | bytes 131104 | tf_op jit(solution)/shard_map/ppermute | solution.py:311
  14.6 0.7 collective-permute-start.4
  15.3 0.0 collective-permute-done.4.beside
  15.3 6.0 %collective-permute-start.5 = (f32[4,4096]{1,0:T(4,128)S(1)}, f32[4,4096]{1,0:T(4,128)S(1)}, u32[]{:S(2)}, u32[]{:S(2)}) collective-permute-start(f32[4,4096]{1,0:T(4,128)S(1)} %collective-permute-done.4.beside), channel_id=1, source_target_pairs={{0,1},{1,0},{2,3},{3,2},{4,5},{5,4},{6,7},{7,6},{8,9},{9,8},{10,11... | collective-permute-start | bytes 196616 | tf_op jit(solution)/shard_map/ppermute | solution.py:311
  21.3 0.9 %collective-permute-done.5.relayed = f32[4,4096]{1,0:T(4,128)S(1)} collective-permute-done((f32[4,4096]{1,0:T(4,128)S(1)}, f32[4,4096]{1,0:T(4,128)S(1)}, u32[]{:S(2)}, u32[]{:S(2)}) %collective-permute-start.5) | collective-permute-done | bytes 65568 | tf_op jit(solution)/shard_map/ppermute | solution.py:311
  22.2 0.8 %shard_map.79 = (f32[8,4096]{1,0:T(8,128)S(1)}, bf16[64,4096]{1,0:T(8,128)(2,1)S(1)}) custom-call(s32[1]{0:T(128)} %bitcast.slab_ref, f32[8,4096]{1,0:T(8,128)S(1)} %get-tuple-element.26.mine, f32[8,4096]{1,0:T(8,128)S(1)} %collective-permute-done.3.mate, f32[4,4096]{1,0:T(4,128)S(1)} %collective-permute-done.4.beside, ...), custom_call_target="tpu_custom_call" | custom-call | tf_op jit(solution)/shard_map/pallas_call | solution.py:283
  23.0 0.4 collective-permute-start.6
  23.5 1.0 %collective-permute-done.6.mate = f32[8,4096]{1,0:T(8,128)S(1)} collective-permute-done((f32[8,4096]{1,0:T(8,128)S(1)}, f32[8,4096]{1,0:T(8,128)S(1)}, u32[]{:S(2)}, u32[]{:S(2)}) %collective-permute-start.6) | collective-permute-done | bytes 131104 | tf_op jit(solution)/shard_map/ppermute | solution.py:311
  24.5 0.4 collective-permute-start.8
  24.9 0.7 collective-permute-start.9
  25.6 0.7 collective-permute-start.7
  26.3 0.0 collective-permute-done.7.beside
  26.3 0.2 collective-permute-done.8.mate_maps
  26.5 1.7 %shard_map.82 = (f32[16,16,128]{2,1,0:T(8,128)}, f32[64,128]{1,0:T(8,128)}) custom-call(s32[1]{0:T(128)} %bitcast.slab_ref, f32[8,4096]{1,0:T(8,128)S(1)} %get-tuple-element.28.mine, f32[8,4096]{1,0:T(8,128)S(1)} %collective-permute-done.6.mate, f32[4,4096]{1,0:T(4,128)S(1)} %collective-permute-done.7.beside, bf16[64,4096]{1,0:T(8,128)(2,1)S(1)} %get-tuple-element.30.maps, ...), custom_call_target="tpu_custom_call" | custom-call | tf_op jit(solution)/shard_map/pallas_call | solution.py:283
  28.2 22.5 %all-to-all-start = ((f32[16,16,128]{2,1,0:T(8,128)}), f32[16,16,128]{2,1,0:T(8,128)S(1)}, u32[]{:S(2)}, u32[]{:S(2)}) async-start(f32[16,16,128]{2,1,0:T(8,128)} %get-tuple-element.32), calls=%async_computation | async-start | bytes 262144 | tf_op jit(solution)/shard_map/all_to_all | solution.py:375
  50.6 0.0 collective-permute-done.9.beside_maps
  50.6 7.9 %all-to-all-done.shares = f32[16,16,128]{2,1,0:T(8,128)S(1)} async-done(((f32[16,16,128]{2,1,0:T(8,128)}), f32[16,16,128]{2,1,0:T(8,128)S(1)}, u32[]{:S(2)}, u32[]{:S(2)}) %all-to-all-start) | async-done | bytes 131104 | tf_op jit(solution)/shard_map/all_to_all | solution.py:375
  58.5 2.0 %shard_map.83 = (f32[32,64]{1,0:T(8,128)}, f32[16,128]{1,0:T(8,128)}) custom-call(s32[1]{0:T(128)} %bitcast.slab_ref, f32[16,16,128]{2,1,0:T(8,128)S(1)} %all-to-all-done.shares, bf16[64,4096]{1,0:T(8,128)(2,1)S(1)} %get-tuple-element.30.maps, bf16[64,4096]{1,0:T(8,128)(2,1)S(1)} %collective-permute-done.8.mate_maps, ...), custom_call_target="tpu_custom_call" | custom-call | tf_op jit(solution)/shard_map/pallas_call | solution.py:283
  60.5 3.4 %all-to-all-start.1 = ((f32[16,1,128]{2,1,0:T(1,128)}), f32[16,1,128]{2,1,0:T(1,128)S(1)}, u32[]{:S(2)}, u32[]{:S(2)}) async-start(f32[16,1,128]{2,1,0:T(1,128)} %bitcast.6), calls=%async_computation.1 | async-start | bytes 16384 | tf_op jit(solution)/shard_map/all_to_all | solution.py:382
  64.0 1.9 %shard_map.81 = bf16[2048,128]{1,0:T(8,128)(2,1)} custom-call(bf16[64,4096]{1,0:T(8,128)(2,1)S(1)} %get-tuple-element.30.maps), custom_call_target="tpu_custom_call" | custom-call | tf_op jit(solution)/shard_map/pallas_call | solution.py:283
  65.9 4.5 %all-to-all-done.1 = f32[16,1,128]{2,1,0:T(1,128)S(1)} async-done(((f32[16,1,128]{2,1,0:T(1,128)}), f32[16,1,128]{2,1,0:T(1,128)S(1)}, u32[]{:S(2)}, u32[]{:S(2)}) %all-to-all-start.1) | async-done | bytes 8224 | tf_op jit(solution)/shard_map/all_to_all | solution.py:382
  70.4 0.6 slice_reduce_fusion
  (3 shorter events, 0.1 us)
Async XLA Ops:
  2.8 1.5 %collective-permute-start = (f32[8,4096]{1,0:T(8,128)S(1)}, f32[8,4096]{1,0:T(8,128)S(1)}, u32[]{:S(2)}, u32[]{:S(2)}) collective-permute-start(f32[8,4096]{1,0:T(8,128)S(1)} %get-tuple-element.20.mine), channel_id=1, source_target_pairs={{0,1},{1,0},{2,3},{3,2},{4,5},{5,4},{6,7},{7,6},{8,9},{9,8},{10,11... | collective-permute-start | bytes 393224 | tf_op jit(solution)/shard_map/ppermute | solution.py:311
  4.4 0.7 collective-permute-start.1
  5.1 7.1 %collective-permute-start.2 = (f32[4,4096]{1,0:T(4,128)S(1)}, f32[4,4096]{1,0:T(4,128)S(1)}, u32[]{:S(2)}, u32[]{:S(2)}) collective-permute-start(f32[4,4096]{1,0:T(4,128)S(1)} %collective-permute-done.1.beside), channel_id=1, source_target_pairs={{0,1},{1,0},{2,3},{3,2},{4,5},{5,4},{6,7},{7,6},{8,9},{9,8},{10,11... | collective-permute-start | bytes 196616 | tf_op jit(solution)/shard_map/ppermute | solution.py:311
  13.2 1.4 %collective-permute-start.3 = (f32[8,4096]{1,0:T(8,128)S(1)}, f32[8,4096]{1,0:T(8,128)S(1)}, u32[]{:S(2)}, u32[]{:S(2)}) collective-permute-start(f32[8,4096]{1,0:T(8,128)S(1)} %get-tuple-element.26.mine), channel_id=1, source_target_pairs={{0,1},{1,0},{2,3},{3,2},{4,5},{5,4},{6,7},{7,6},{8,9},{9,8},{10,11... | collective-permute-start | bytes 393224 | tf_op jit(solution)/shard_map/ppermute | solution.py:311
  14.6 0.7 collective-permute-start.4
  15.3 6.9 %collective-permute-start.5 = (f32[4,4096]{1,0:T(4,128)S(1)}, f32[4,4096]{1,0:T(4,128)S(1)}, u32[]{:S(2)}, u32[]{:S(2)}) collective-permute-start(f32[4,4096]{1,0:T(4,128)S(1)} %collective-permute-done.4.beside), channel_id=1, source_target_pairs={{0,1},{1,0},{2,3},{3,2},{4,5},{5,4},{6,7},{7,6},{8,9},{9,8},{10,11... | collective-permute-start | bytes 196616 | tf_op jit(solution)/shard_map/ppermute | solution.py:311
  23.0 1.4 %collective-permute-start.6 = (f32[8,4096]{1,0:T(8,128)S(1)}, f32[8,4096]{1,0:T(8,128)S(1)}, u32[]{:S(2)}, u32[]{:S(2)}) collective-permute-start(f32[8,4096]{1,0:T(8,128)S(1)} %get-tuple-element.28.mine), channel_id=1, source_target_pairs={{0,1},{1,0},{2,3},{3,2},{4,5},{5,4},{6,7},{7,6},{8,9},{9,8},{10,11... | collective-permute-start | bytes 393224 | tf_op jit(solution)/shard_map/ppermute | solution.py:311
  24.5 2.0 %collective-permute-start.8 = (bf16[64,4096]{1,0:T(8,128)(2,1)S(1)}, bf16[64,4096]{1,0:T(8,128)(2,1)S(1)}, u32[]{:S(2)}, u32[]{:S(2)}) collective-permute-start(bf16[64,4096]{1,0:T(8,128)(2,1)S(1)} %get-tuple-element.30.maps), channel_id=1, source_target_pairs={{0,1},{1,0},{2,3},{3,2},{4,5},{5,4},{6,7},{7,6},{8,9},{9,8},{10,11... | collective-permute-start | bytes 1572872 | tf_op jit(solution)/shard_map/ppermute | solution.py:311
  24.9 25.7 %collective-permute-start.9 = (bf16[64,4096]{1,0:T(8,128)(2,1)S(1)}, bf16[64,4096]{1,0:T(8,128)(2,1)S(1)}, u32[]{:S(2)}, u32[]{:S(2)}) collective-permute-start(bf16[64,4096]{1,0:T(8,128)(2,1)S(1)} %get-tuple-element.30.maps), channel_id=1, source_target_pairs={{1,2},{3,4},{5,6},{7,8},{9,10},{11,12},{13,14},{2,1},{4,3},{6,5},{... | collective-permute-start | bytes 1572872 | tf_op jit(solution)/shard_map/ppermute | solution.py:314
  25.6 0.7 collective-permute-start.7
  28.2 30.4 %all-to-all-start = ((f32[16,16,128]{2,1,0:T(8,128)}), f32[16,16,128]{2,1,0:T(8,128)S(1)}, u32[]{:S(2)}, u32[]{:S(2)}) async-start(f32[16,16,128]{2,1,0:T(8,128)} %get-tuple-element.32), calls=%async_computation | async-start | bytes 262144 | tf_op jit(solution)/shard_map/all_to_all | solution.py:375
  60.5 9.8 %all-to-all-start.1 = ((f32[16,1,128]{2,1,0:T(1,128)}), f32[16,1,128]{2,1,0:T(1,128)S(1)}, u32[]{:S(2)}, u32[]{:S(2)}) async-start(f32[16,1,128]{2,1,0:T(1,128)} %bitcast.6), calls=%async_computation.1 | async-start | bytes 16384 | tf_op jit(solution)/shard_map/all_to_all | solution.py:382

commit v3 on v2

--- a/solution.py
+++ b/solution.py
@@ -92,12 +92,14 @@
 
 def gather_resid(slab, slabs, mine, mate, beside, relayed, height, breadth, visit):
     offset = plane_offset(slab, (8, breadth))
-    from_beside = sent_range(slab, offset)
-    from_relay = offset == 4 * (1 - (slab & 1))
+    odd = slab & 1
+    edge = slab + 1 - 2 * odd
+    from_beside = sent_range(slab, offset) & (slab > 0) & (slab < slabs - 1)
+    from_relay = (offset == 4 * (1 - odd)) & (edge > 0) & (edge < slabs - 1)
     plane = 2 * slab - 1 + offset
     valid = (offset < 5) & (plane >= 0) & (plane < 2 * slabs)
     if relayed is None:
-        valid &= ~from_relay
+        valid &= offset != 4 * (1 - odd)
     for y in range(height):
         cols = slice(y * breadth, (y + 1) * breadth)
         near = beside[:, cols]
@@ -254,7 +256,7 @@
         shares[j] = packed
 
 
-def probe_kernel(height, breadth, slab_ref, shares, maps, mate_maps, beside_maps, descent_out, norms, products, folded):
+def probe_kernel(height, breadth, slabs, slab_ref, shares, maps, mate_maps, beside_maps, descent_out, norms, products, folded):
     slab = slab_ref[0]
     packed = jnp.sum(shares[...], axis=0)
     descent = jnp.concatenate([packed[:, :64], packed[:, 64:]], axis=0)
@@ -268,10 +270,11 @@
     def emit(y, total):
         folded[...] += jnp.where(own, total * total, 0.0)
 
+    beside_bank = bank_cols(half, slab - 1 + 2 * odd)
     pairs = [
         (bank_cols(half, slab), maps),
         (bank_cols(half, slab + 1 - 2 * odd), mate_maps),
-        (bank_cols(half, slab - 1 + 2 * odd), beside_maps),
+        (jnp.where((slab > 0) & (slab < slabs - 1), beside_bank, jnp.zeros_like(beside_bank)), beside_maps),
     ]
     spread(pairs, products, height, breadth, emit)
     total = jnp.sum(jnp.sum(folded[...], axis=1, keepdims=True), axis=0, keepdims=True)
@@ -304,14 +307,16 @@
     )
 
     mates = [(i, i ^ 1) for i in range(slabs)]
-    besides = [(i, i + 1) for i in range(1, slabs - 1, 2)]
+    parts = lax.axis_size("vol")
+    besides = [(v * slabs + i, v * slabs + i + 1) for v in range(parts) for i in range(1, slabs - 1, 2)]
+    besides += [(v * slabs + i, (v + 1) * slabs + i) for v in range(0, parts - 1, 2) for i in (0, slabs - 1)]
     besides += [(j, i) for i, j in besides]
 
     def to_mate(x):
         return lax.ppermute(x, "gz", mates)
 
     def to_beside(x):
-        return lax.ppermute(x, "gz", besides)
+        return lax.ppermute(x, ("vol", "gz"), besides)
 
     share_shape = ((8, size), F32)
     maps_shape = ((2 * atom_count, size), BF16)
@@ -374,7 +379,7 @@
     )
     shares = lax.all_to_all(shares, "gz", 0, 0)
     descent, norms = call(
-        functools.partial(probe_kernel, height, breadth),
+        functools.partial(probe_kernel, height, breadth, slabs),
         [((atom_count, 64), F32), ((slabs, 128), F32)],
         (slab, shares, maps, mate_maps, beside_maps),
         [products, ((8, breadth), F32)],

time: 71.4 us -> 65.8 us (0.922)
  starting transfers between devices: 42.5 us -> 24 us
  waiting for transfers between devices: 17.4 us -> 30.4 us
    ppermute x6, starting transfers between devices: 13.9 us -> 1.46 us  [to_mate(): return lax.ppermute(x, 'gz', mates)]
    ppermute x4, waiting for transfers between devices: 0.01 us -> 12.3 us  [to_beside(): return lax.ppermute(x, ('vol', 'gz'), besides)]
    all_to_all x1, starting transfers between devices: 22.5 us -> 12.1 us  [per_device(): shares = lax.all_to_all(shares, 'gz', 0, 0)]
    ppermute x4, starting transfers between devices: 2.68 us -> 7.02 us  [to_beside(): return lax.ppermute(x, ('vol', 'gz'), besides)]
  transfers between devices with their start and end apart: 12 -> 12, of which waited for: 8 -> 10; matrix products, arithmetic and copies ran while one was open for 0% -> 0% of each run, Pallas kernels for 5% -> 5%
where the time goes in v3:
time: 65.8 us; the launch traced here: 65.5 us
  waiting for transfers between devices  30.4 us (46%)
  starting transfers between devices  24 us (36%)
  Pallas kernels  9.8 us (15%)
  between operations  0.7 us (1%)
    ppermute x4, waiting for transfers between devices, to_beside(): return lax.ppermute(x, ('vol', 'gz'), besides)  12.3 us
    all_to_all x1, starting transfers between devices, per_device(): shares = lax.all_to_all(shares, 'gz', 0, 0)  12.1 us
    pallas_call x9, Pallas kernels, call(): pl.pallas_call(kernel, out_shape=[jax.ShapeDtypeStruct(shape, dtype) for...  9.8 us
    all_to_all x1, waiting for transfers between devices, per_device(): shares = lax.all_to_all(shares, 'gz', 0, 0)  7.89 us
    ppermute x4, starting transfers between devices, to_beside(): return lax.ppermute(x, ('vol', 'gz'), besides)  7.02 us
    ppermute x6, waiting for transfers between devices, to_mate(): return lax.ppermute(x, 'gz', mates)  5.65 us
    all_to_all x1, waiting for transfers between devices, per_device(): norms = lax.all_to_all(norms.reshape(slabs, 1, 128), 'gz', 0, 0)  4.51 us
    all_to_all x1, starting transfers between devices, per_device(): norms = lax.all_to_all(norms.reshape(slabs, 1, 128), 'gz', 0, 0)  3.43 us
  transfers between devices with their start and end apart: 12, of which 10 were waited for; matrix products, arithmetic and copies ran while one was open for 0% of the time, Pallas kernels for 5%

profile of v3, /device:TPU:0, one launch (start us, length us, event | category | flops | bytes accessed | tf_op | source)
XLA Modules:
  0.0 65.5 jit_solution(9969670865217868020)
XLA Ops:
  0.6 2.2 %shard_map.75 = (f32[8,4096]{1,0:T(8,128)S(1)}, bf16[64,4096]{1,0:T(8,128)(2,1)S(1)}, bf16[64,128]{1,0:T(8,128)(2,1)S(1)}, bf16[128,64]{1,0:T(8,128)(2,1)S(1)}, ...) custom-call(s32[1]{0:T(128)} %bitcast.slab_ref, bf16[2048,128]{1,0:T(8,128)(2,1)} %bitcast.10, f32[64,128]{1,0:T(8,128)} %bitcast.12, ...), custom_call_target="tpu_custom_call" | custom-call | tf_op jit(solution)/shard_map/pallas_call | solution.py:286
  2.8 0.6 collective-permute-start
  3.4 1.0 %collective-permute-done.mate = f32[8,4096]{1,0:T(8,128)S(1)} collective-permute-done((f32[8,4096]{1,0:T(8,128)S(1)}, f32[8,4096]{1,0:T(8,128)S(1)}, u32[]{:S(2)}, u32[]{:S(2)}) %collective-permute-start) | collective-permute-done | bytes 131104 | tf_op jit(solution)/shard_map/ppermute | solution.py:316
  4.4 2.9 %collective-permute-start.1 = (f32[4,4096]{1,0:T(4,128)S(1)}, f32[4,4096]{1,0:T(4,128)S(1)}, u32[]{:S(2)}, u32[]{:S(2)}) collective-permute-start(f32[4,4096]{1,0:T(4,128)S(1)} %shard_map.76), channel_id=1, source_target_pairs={{1,2},{3,4},{5,6},{7,8},{9,10},{11,12},{13,14},{17,18},{19,20},{21... | collective-permute-start | bytes 196616 | tf_op jit(solution)/shard_map/ppermute | solution.py:319
  7.3 2.2 %collective-permute-done.1.beside = f32[4,4096]{1,0:T(4,128)S(1)} collective-permute-done((f32[4,4096]{1,0:T(4,128)S(1)}, f32[4,4096]{1,0:T(4,128)S(1)}, u32[]{:S(2)}, u32[]{:S(2)}) %collective-permute-start.1) | collective-permute-done | bytes 65568 | tf_op jit(solution)/shard_map/ppermute | solution.py:319
  9.6 0.1 collective-permute-start.2
  9.7 1.1 %collective-permute-done.2.relayed = f32[4,4096]{1,0:T(4,128)S(1)} collective-permute-done((f32[4,4096]{1,0:T(4,128)S(1)}, f32[4,4096]{1,0:T(4,128)S(1)}, u32[]{:S(2)}, u32[]{:S(2)}) %collective-permute-start.2) | collective-permute-done | bytes 65568 | tf_op jit(solution)/shard_map/ppermute | solution.py:316
  10.8 1.1 %shard_map.77 = (f32[8,4096]{1,0:T(8,128)S(1)}, bf16[64,4096]{1,0:T(8,128)(2,1)S(1)}) custom-call(s32[1]{0:T(128)} %bitcast.slab_ref, f32[8,4096]{1,0:T(8,128)S(1)} %get-tuple-element.20.mine, f32[8,4096]{1,0:T(8,128)S(1)} %collective-permute-done.mate, f32[4,4096]{1,0:T(4,128)S(1)} %collective-permute-done.1.beside, ...), custom_call_target="tpu_custom_call" | custom-call | tf_op jit(solution)/shard_map/pallas_call | solution.py:286
  11.9 0.2 collective-permute-start.3
  12.1 1.2 %collective-permute-done.3.mate = f32[8,4096]{1,0:T(8,128)S(1)} collective-permute-done((f32[8,4096]{1,0:T(8,128)S(1)}, f32[8,4096]{1,0:T(8,128)S(1)}, u32[]{:S(2)}, u32[]{:S(2)}) %collective-permute-start.3) | collective-permute-done | bytes 131104 | tf_op jit(solution)/shard_map/ppermute | solution.py:316
  13.3 2.1 %collective-permute-start.4 = (f32[4,4096]{1,0:T(4,128)S(1)}, f32[4,4096]{1,0:T(4,128)S(1)}, u32[]{:S(2)}, u32[]{:S(2)}) collective-permute-start(f32[4,4096]{1,0:T(4,128)S(1)} %shard_map.78), channel_id=1, source_target_pairs={{1,2},{3,4},{5,6},{7,8},{9,10},{11,12},{13,14},{17,18},{19,20},{21... | collective-permute-start | bytes 196616 | tf_op jit(solution)/shard_map/ppermute | solution.py:319
  15.4 2.2 %collective-permute-done.4.beside = f32[4,4096]{1,0:T(4,128)S(1)} collective-permute-done((f32[4,4096]{1,0:T(4,128)S(1)}, f32[4,4096]{1,0:T(4,128)S(1)}, u32[]{:S(2)}, u32[]{:S(2)}) %collective-permute-start.4) | collective-permute-done | bytes 65568 | tf_op jit(solution)/shard_map/ppermute | solution.py:319
  17.7 0.1 collective-permute-start.5
  17.8 1.1 %collective-permute-done.5.relayed = f32[4,4096]{1,0:T(4,128)S(1)} collective-permute-done((f32[4,4096]{1,0:T(4,128)S(1)}, f32[4,4096]{1,0:T(4,128)S(1)}, u32[]{:S(2)}, u32[]{:S(2)}) %collective-permute-start.5) | collective-permute-done | bytes 65568 | tf_op jit(solution)/shard_map/ppermute | solution.py:316
  18.9 0.9 %shard_map.79 = (f32[8,4096]{1,0:T(8,128)S(1)}, bf16[64,4096]{1,0:T(8,128)(2,1)S(1)}) custom-call(s32[1]{0:T(128)} %bitcast.slab_ref, f32[8,4096]{1,0:T(8,128)S(1)} %get-tuple-element.26.mine, f32[8,4096]{1,0:T(8,128)S(1)} %collective-permute-done.3.mate, f32[4,4096]{1,0:T(4,128)S(1)} %collective-permute-done.4.beside, ...), custom_call_target="tpu_custom_call" | custom-call | tf_op jit(solution)/shard_map/pallas_call | solution.py:286
  19.8 0.2 collective-permute-start.6
  20.0 1.2 %collective-permute-done.6.mate = f32[8,4096]{1,0:T(8,128)S(1)} collective-permute-done((f32[8,4096]{1,0:T(8,128)S(1)}, f32[8,4096]{1,0:T(8,128)S(1)}, u32[]{:S(2)}, u32[]{:S(2)}) %collective-permute-start.6) | collective-permute-done | bytes 131104 | tf_op jit(solution)/shard_map/ppermute | solution.py:316
  21.2 0.2 collective-permute-start.8
  21.4 2.0 %collective-permute-start.9 = (bf16[64,4096]{1,0:T(8,128)(2,1)S(1)}, bf16[64,4096]{1,0:T(8,128)(2,1)S(1)}, u32[]{:S(2)}, u32[]{:S(2)}) collective-permute-start(bf16[64,4096]{1,0:T(8,128)(2,1)S(1)} %get-tuple-element.30.maps), channel_id=1, source_target_pairs={{1,2},{3,4},{5,6},{7,8},{9,10},{11,12},{13,14},{17,18},{19,20},{21... | collective-permute-start | bytes 1572872 | tf_op jit(solution)/shard_map/ppermute | solution.py:319
  23.4 0.0 collective-permute-start.7
  23.5 7.8 %collective-permute-done.7.beside = f32[4,4096]{1,0:T(4,128)S(1)} collective-permute-done((f32[4,4096]{1,0:T(4,128)S(1)}, f32[4,4096]{1,0:T(4,128)S(1)}, u32[]{:S(2)}, u32[]{:S(2)}) %collective-permute-start.7) | collective-permute-done | bytes 65568 | tf_op jit(solution)/shard_map/ppermute | solution.py:319
  31.3 0.0 collective-permute-done.8.mate_maps
  31.3 1.7 %shard_map.82 = (f32[16,16,128]{2,1,0:T(8,128)}, f32[64,128]{1,0:T(8,128)}) custom-call(s32[1]{0:T(128)} %bitcast.slab_ref, f32[8,4096]{1,0:T(8,128)S(1)} %get-tuple-element.28.mine, f32[8,4096]{1,0:T(8,128)S(1)} %collective-permute-done.6.mate, f32[4,4096]{1,0:T(4,128)S(1)} %collective-permute-done.7.beside, bf16[64,4096]{1,0:T(8,128)(2,1)S(1)} %get-tuple-element.30.maps, ...), custom_call_target="tpu_custom_call" | custom-call | tf_op jit(solution)/shard_map/pallas_call | solution.py:286
  33.0 12.1 %all-to-all-start = ((f32[16,16,128]{2,1,0:T(8,128)}), f32[16,16,128]{2,1,0:T(8,128)S(1)}, u32[]{:S(2)}, u32[]{:S(2)}) async-start(f32[16,16,128]{2,1,0:T(8,128)} %get-tuple-element.32), calls=%async_computation | async-start | bytes 262144 | tf_op jit(solution)/shard_map/all_to_all | solution.py:380
  45.1 0.0 collective-permute-done.9.beside_maps
  45.1 7.9 %all-to-all-done.shares = f32[16,16,128]{2,1,0:T(8,128)S(1)} async-done(((f32[16,16,128]{2,1,0:T(8,128)}), f32[16,16,128]{2,1,0:T(8,128)S(1)}, u32[]{:S(2)}, u32[]{:S(2)}) %all-to-all-start) | async-done | bytes 131104 | tf_op jit(solution)/shard_map/all_to_all | solution.py:380
  53.0 2.0 %shard_map.83 = (f32[32,64]{1,0:T(8,128)}, f32[16,128]{1,0:T(8,128)}) custom-call(s32[1]{0:T(128)} %bitcast.slab_ref, f32[16,16,128]{2,1,0:T(8,128)S(1)} %all-to-all-done.shares, bf16[64,4096]{1,0:T(8,128)(2,1)S(1)} %get-tuple-element.30.maps, bf16[64,4096]{1,0:T(8,128)(2,1)S(1)} %collective-permute-done.8.mate_maps, ...), custom_call_target="tpu_custom_call" | custom-call | tf_op jit(solution)/shard_map/pallas_call | solution.py:286
  55.0 3.4 %all-to-all-start.1 = ((f32[16,1,128]{2,1,0:T(1,128)}), f32[16,1,128]{2,1,0:T(1,128)S(1)}, u32[]{:S(2)}, u32[]{:S(2)}) async-start(f32[16,1,128]{2,1,0:T(1,128)} %bitcast.6), calls=%async_computation.1 | async-start | bytes 16384 | tf_op jit(solution)/shard_map/all_to_all | solution.py:387
  58.5 1.9 %shard_map.81 = bf16[2048,128]{1,0:T(8,128)(2,1)} custom-call(bf16[64,4096]{1,0:T(8,128)(2,1)S(1)} %get-tuple-element.30.maps), custom_call_target="tpu_custom_call" | custom-call | tf_op jit(solution)/shard_map/pallas_call | solution.py:286
  60.3 4.5 %all-to-all-done.1 = f32[16,1,128]{2,1,0:T(1,128)S(1)} async-done(((f32[16,1,128]{2,1,0:T(1,128)}), f32[16,1,128]{2,1,0:T(1,128)S(1)}, u32[]{:S(2)}, u32[]{:S(2)}) %all-to-all-start.1) | async-done | bytes 8224 | tf_op jit(solution)/shard_map/all_to_all | solution.py:387
  64.9 0.6 slice_reduce_fusion
  (3 shorter events, 0.1 us)
Async XLA Ops:
  2.8 1.5 %collective-permute-start = (f32[8,4096]{1,0:T(8,128)S(1)}, f32[8,4096]{1,0:T(8,128)S(1)}, u32[]{:S(2)}, u32[]{:S(2)}) collective-permute-start(f32[8,4096]{1,0:T(8,128)S(1)} %get-tuple-element.20.mine), channel_id=1, source_target_pairs={{0,1},{1,0},{2,3},{3,2},{4,5},{5,4},{6,7},{7,6},{8,9},{9,8},{10,11... | collective-permute-start | bytes 393224 | tf_op jit(solution)/shard_map/ppermute | solution.py:316
  4.4 5.1 %collective-permute-start.1 = (f32[4,4096]{1,0:T(4,128)S(1)}, f32[4,4096]{1,0:T(4,128)S(1)}, u32[]{:S(2)}, u32[]{:S(2)}) collective-permute-start(f32[4,4096]{1,0:T(4,128)S(1)} %shard_map.76), channel_id=1, source_target_pairs={{1,2},{3,4},{5,6},{7,8},{9,10},{11,12},{13,14},{17,18},{19,20},{21... | collective-permute-start | bytes 196616 | tf_op jit(solution)/shard_map/ppermute | solution.py:319
  9.6 1.3 %collective-permute-start.2 = (f32[4,4096]{1,0:T(4,128)S(1)}, f32[4,4096]{1,0:T(4,128)S(1)}, u32[]{:S(2)}, u32[]{:S(2)}) collective-permute-start(f32[4,4096]{1,0:T(4,128)S(1)} %collective-permute-done.1.beside), channel_id=1, source_target_pairs={{0,1},{1,0},{2,3},{3,2},{4,5},{5,4},{6,7},{7,6},{8,9},{9,8},{10,11... | collective-permute-start | bytes 196616 | tf_op jit(solution)/shard_map/ppermute | solution.py:316
  11.9 1.4 %collective-permute-start.3 = (f32[8,4096]{1,0:T(8,128)S(1)}, f32[8,4096]{1,0:T(8,128)S(1)}, u32[]{:S(2)}, u32[]{:S(2)}) collective-permute-start(f32[8,4096]{1,0:T(8,128)S(1)} %get-tuple-element.26.mine), channel_id=1, source_target_pairs={{0,1},{1,0},{2,3},{3,2},{4,5},{5,4},{6,7},{7,6},{8,9},{9,8},{10,11... | collective-permute-start | bytes 393224 | tf_op jit(solution)/shard_map/ppermute | solution.py:316
  13.3 4.3 %collective-permute-start.4 = (f32[4,4096]{1,0:T(4,128)S(1)}, f32[4,4096]{1,0:T(4,128)S(1)}, u32[]{:S(2)}, u32[]{:S(2)}) collective-permute-start(f32[4,4096]{1,0:T(4,128)S(1)} %shard_map.78), channel_id=1, source_target_pairs={{1,2},{3,4},{5,6},{7,8},{9,10},{11,12},{13,14},{17,18},{19,20},{21... | collective-permute-start | bytes 196616 | tf_op jit(solution)/shard_map/ppermute | solution.py:319
  17.7 1.3 %collective-permute-start.5 = (f32[4,4096]{1,0:T(4,128)S(1)}, f32[4,4096]{1,0:T(4,128)S(1)}, u32[]{:S(2)}, u32[]{:S(2)}) collective-permute-start(f32[4,4096]{1,0:T(4,128)S(1)} %collective-permute-done.4.beside), channel_id=1, source_target_pairs={{0,1},{1,0},{2,3},{3,2},{4,5},{5,4},{6,7},{7,6},{8,9},{9,8},{10,11... | collective-permute-start | bytes 196616 | tf_op jit(solution)/shard_map/ppermute | solution.py:316
  19.8 1.4 %collective-permute-start.6 = (f32[8,4096]{1,0:T(8,128)S(1)}, f32[8,4096]{1,0:T(8,128)S(1)}, u32[]{:S(2)}, u32[]{:S(2)}) collective-permute-start(f32[8,4096]{1,0:T(8,128)S(1)} %get-tuple-element.28.mine), channel_id=1, source_target_pairs={{0,1},{1,0},{2,3},{3,2},{4,5},{5,4},{6,7},{7,6},{8,9},{9,8},{10,11... | collective-permute-start | bytes 393224 | tf_op jit(solution)/shard_map/ppermute | solution.py:316
  21.2 10.1 %collective-permute-start.8 = (bf16[64,4096]{1,0:T(8,128)(2,1)S(1)}, bf16[64,4096]{1,0:T(8,128)(2,1)S(1)}, u32[]{:S(2)}, u32[]{:S(2)}) collective-permute-start(bf16[64,4096]{1,0:T(8,128)(2,1)S(1)} %get-tuple-element.30.maps), channel_id=1, source_target_pairs={{0,1},{1,0},{2,3},{3,2},{4,5},{5,4},{6,7},{7,6},{8,9},{9,8},{10,11... | collective-permute-start | bytes 1572872 | tf_op jit(solution)/shard_map/ppermute | solution.py:316
  21.4 23.7 %collective-permute-start.9 = (bf16[64,4096]{1,0:T(8,128)(2,1)S(1)}, bf16[64,4096]{1,0:T(8,128)(2,1)S(1)}, u32[]{:S(2)}, u32[]{:S(2)}) collective-permute-start(bf16[64,4096]{1,0:T(8,128)(2,1)S(1)} %get-tuple-element.30.maps), channel_id=1, source_target_pairs={{1,2},{3,4},{5,6},{7,8},{9,10},{11,12},{13,14},{17,18},{19,20},{21... | collective-permute-start | bytes 1572872 | tf_op jit(solution)/shard_map/ppermute | solution.py:319
  23.4 7.9 %collective-permute-start.7 = (f32[4,4096]{1,0:T(4,128)S(1)}, f32[4,4096]{1,0:T(4,128)S(1)}, u32[]{:S(2)}, u32[]{:S(2)}) collective-permute-start(f32[4,4096]{1,0:T(4,128)S(1)} %shard_map.80), channel_id=1, source_target_pairs={{1,2},{3,4},{5,6},{7,8},{9,10},{11,12},{13,14},{17,18},{19,20},{21... | collective-permute-start | bytes 196616 | tf_op jit(solution)/shard_map/ppermute | solution.py:319
  33.0 20.0 %all-to-all-start = ((f32[16,16,128]{2,1,0:T(8,128)}), f32[16,16,128]{2,1,0:T(8,128)S(1)}, u32[]{:S(2)}, u32[]{:S(2)}) async-start(f32[16,16,128]{2,1,0:T(8,128)} %get-tuple-element.32), calls=%async_computation | async-start | bytes 262144 | tf_op jit(solution)/shard_map/all_to_all | solution.py:380
  55.0 9.8 %all-to-all-start.1 = ((f32[16,1,128]{2,1,0:T(1,128)}), f32[16,1,128]{2,1,0:T(1,128)S(1)}, u32[]{:S(2)}, u32[]{:S(2)}) async-start(f32[16,1,128]{2,1,0:T(1,128)} %bitcast.6), calls=%async_computation.1 | async-start | bytes 16384 | tf_op jit(solution)/shard_map/all_to_all | solution.py:387

commit v4 on v3

--- a/solution.py
+++ b/solution.py
@@ -219,7 +219,7 @@
 
 
 def descent_kernel(
-    height, breadth, slabs, slab_ref, mine, mate, beside, maps, mate_maps, shares, resid_out, unfolded, planes
+    height, breadth, slabs, slab_ref, mine, mate, beside, maps, mate_maps, packed, resid_out, unfolded, planes
 ):
     slab = slab_ref[0]
     odd = slab & 1
@@ -251,14 +251,24 @@
                 total += taps_dot(head, pick, ((1,), (0,)))
                 left = left - head.astype(F32)
     half = atom_count // 2
-    packed = jnp.concatenate([total[:half], total[half:]], axis=1)
-    for j in range(slabs):
-        shares[j] = packed
-
-
-def probe_kernel(height, breadth, slabs, slab_ref, shares, maps, mate_maps, beside_maps, descent_out, norms, products, folded):
+    packed[...] = jnp.concatenate([total[:half], total[half:]], axis=1)
+
+
+def sum_refs(refs):
+    terms = [ref[...] for ref in refs]
+    while len(terms) > 1:
+        terms = [sum(terms[k + 1 : k + 2], terms[k]) for k in range(0, len(terms), 2)]
+    return terms[0]
+
+
+def sum_kernel(*refs):
+    refs[-1][...] = sum_refs(refs[:-1])
+
+
+def probe_kernel(height, breadth, slabs, slab_ref, maps, mate_maps, beside_maps, *rest):
+    *shares, descent_out, norms, products, folded = rest
     slab = slab_ref[0]
-    packed = jnp.sum(shares[...], axis=0)
+    packed = sum_refs(shares)
     descent = jnp.concatenate([packed[:, :64], packed[:, 64:]], axis=0)
     descent_out[...] = descent
     half = descent.astype(BF16)
@@ -371,17 +381,28 @@
     (natural,) = call(
         functools.partial(natural_kernel, height, breadth), [natural_shape], (maps,), [wide], [pltpu.VMEM]
     )
-    shares, residual = call(
+    packed_shape = ((atom_count // 2, 128), F32)
+    packed, residual = call(
         functools.partial(descent_kernel, height, breadth, slabs),
-        [((slabs, atom_count // 2, 128), F32), (tomo.shape, F32)],
+        [packed_shape, (tomo.shape, F32)],
         (slab, mine, mate, beside, maps, mate_maps),
         [unfolded, ((8 * height, breadth), F32)],
     )
-    shares = lax.all_to_all(shares, "gz", 0, 0)
+    shares = [packed]
+    stride = 1
+    while stride < slabs:
+        if len(shares) > 1:
+            shares = call(sum_kernel, [packed_shape], shares, (), [pltpu.VMEM] * len(shares))
+        shares = [*shares] + [
+            lax.ppermute(shares[0], "gz", [(i, i ^ (k * stride)) for i in range(slabs)])
+            for k in (3, 2, 1)
+            if k * stride < slabs
+        ]
+        stride *= 4
     descent, norms = call(
         functools.partial(probe_kernel, height, breadth, slabs),
         [((atom_count, 64), F32), ((slabs, 128), F32)],
-        (slab, shares, maps, mate_maps, beside_maps),
+        (slab, maps, mate_maps, beside_maps, *shares),
         [products, ((8, breadth), F32)],
     )
     norms = lax.all_to_all(norms.reshape(slabs, 1, 128), "gz", 0, 0)

time: 65.8 us -> 66 us (level)
  starting transfers between devices: 24 us -> 26.9 us
  waiting for transfers between devices: 30.4 us -> 28 us
    ppermute x0 -> x6, starting transfers between devices: none -> 13.6 us  [per_device(): lax.ppermute(shares[0], 'gz', [(i, i ^ k * stride) for i in range(slabs)])]
    all_to_all x1 -> x0, starting transfers between devices: 12.1 us -> none  [per_device(): shares = lax.all_to_all(shares, 'gz', 0, 0)]
    all_to_all x1 -> x0, waiting for transfers between devices: 7.89 us -> none  [per_device(): shares = lax.all_to_all(shares, 'gz', 0, 0)]
    ppermute x0 -> x6, waiting for transfers between devices: none -> 5.5 us  [per_device(): lax.ppermute(shares[0], 'gz', [(i, i ^ k * stride) for i in range(slabs)])]
    all_to_all x1, starting transfers between devices: 3.43 us -> 4.78 us  [per_device(): norms = lax.all_to_all(norms.reshape(slabs, 1, 128), 'gz', 0, 0)]
    pallas_call x9 -> x10, Pallas kernels: 9.8 us -> 9.56 us  [call(): pl.pallas_call(kernel, out_shape=[jax.ShapeDtypeStruct(shape, dtype) for...]
  transfers between devices with their start and end apart: 12 -> 17, of which waited for: 10 -> 12; matrix products, arithmetic and copies ran while one was open for 0% -> 0% of each run, Pallas kernels for 5% -> 5%
where the time goes in v4:
time: 66 us; the launch traced here: 65.8 us
  waiting for transfers between devices  28 us (42%)
  starting transfers between devices  26.9 us (41%)
  Pallas kernels  9.56 us (14%)
  between operations  0.69 us (1%)
    ppermute x6, starting transfers between devices, per_device(): lax.ppermute(shares[0], 'gz', [(i, i ^ k * stride) for i in range(slabs)])  13.6 us
    ppermute x4, waiting for transfers between devices, to_beside(): return lax.ppermute(x, ('vol', 'gz'), besides)  12.3 us
    pallas_call x10, Pallas kernels, call(): pl.pallas_call(kernel, out_shape=[jax.ShapeDtypeStruct(shape, dtype) for...  9.56 us
    ppermute x4, starting transfers between devices, to_beside(): return lax.ppermute(x, ('vol', 'gz'), besides)  7.02 us
    ppermute x6, waiting for transfers between devices, to_mate(): return lax.ppermute(x, 'gz', mates)  5.65 us
    ppermute x6, waiting for transfers between devices, per_device(): lax.ppermute(shares[0], 'gz', [(i, i ^ k * stride) for i in range(slabs)])  5.5 us
    all_to_all x1, starting transfers between devices, per_device(): norms = lax.all_to_all(norms.reshape(slabs, 1, 128), 'gz', 0, 0)  4.78 us
    all_to_all x1, waiting for transfers between devices, per_device(): norms = lax.all_to_all(norms.reshape(slabs, 1, 128), 'gz', 0, 0)  4.55 us
  transfers between devices with their start and end apart: 17, of which 12 were waited for; matrix products, arithmetic and copies ran while one was open for 0% of the time, Pallas kernels for 5%

profile of v4, /device:TPU:0, one launch (start us, length us, event | category | flops | bytes accessed | tf_op | source)
XLA Modules:
  0.0 65.8 jit_solution(6752424493940836321)
XLA Ops:
  0.6 2.2 %shard_map.75 = (f32[8,4096]{1,0:T(8,128)S(1)}, bf16[64,4096]{1,0:T(8,128)(2,1)S(1)}, bf16[64,128]{1,0:T(8,128)(2,1)S(1)}, bf16[128,64]{1,0:T(8,128)(2,1)S(1)}, ...) custom-call(s32[1]{0:T(128)} %bitcast.slab_ref, bf16[2048,128]{1,0:T(8,128)(2,1)} %bitcast.10, f32[64,128]{1,0:T(8,128)} %bitcast.12, ...), custom_call_target="tpu_custom_call" | custom-call | tf_op jit(solution)/shard_map/pallas_call | solution.py:296
  2.8 0.6 collective-permute-start
  3.4 1.0 %collective-permute-done.mate = f32[8,4096]{1,0:T(8,128)S(1)} collective-permute-done((f32[8,4096]{1,0:T(8,128)S(1)}, f32[8,4096]{1,0:T(8,128)S(1)}, u32[]{:S(2)}, u32[]{:S(2)}) %collective-permute-start) | collective-permute-done | bytes 131104 | tf_op jit(solution)/shard_map/ppermute | solution.py:326
  4.4 2.9 %collective-permute-start.1 = (f32[4,4096]{1,0:T(4,128)S(1)}, f32[4,4096]{1,0:T(4,128)S(1)}, u32[]{:S(2)}, u32[]{:S(2)}) collective-permute-start(f32[4,4096]{1,0:T(4,128)S(1)} %shard_map.76), channel_id=1, source_target_pairs={{1,2},{3,4},{5,6},{7,8},{9,10},{11,12},{13,14},{17,18},{19,20},{21... | collective-permute-start | bytes 196616 | tf_op jit(solution)/shard_map/ppermute | solution.py:329
  7.3 2.2 %collective-permute-done.1.beside = f32[4,4096]{1,0:T(4,128)S(1)} collective-permute-done((f32[4,4096]{1,0:T(4,128)S(1)}, f32[4,4096]{1,0:T(4,128)S(1)}, u32[]{:S(2)}, u32[]{:S(2)}) %collective-permute-start.1) | collective-permute-done | bytes 65568 | tf_op jit(solution)/shard_map/ppermute | solution.py:329
  9.6 0.1 collective-permute-start.2
  9.7 1.1 %collective-permute-done.2.relayed = f32[4,4096]{1,0:T(4,128)S(1)} collective-permute-done((f32[4,4096]{1,0:T(4,128)S(1)}, f32[4,4096]{1,0:T(4,128)S(1)}, u32[]{:S(2)}, u32[]{:S(2)}) %collective-permute-start.2) | collective-permute-done | bytes 65568 | tf_op jit(solution)/shard_map/ppermute | solution.py:326
  10.8 1.1 %shard_map.77 = (f32[8,4096]{1,0:T(8,128)S(1)}, bf16[64,4096]{1,0:T(8,128)(2,1)S(1)}) custom-call(s32[1]{0:T(128)} %bitcast.slab_ref, f32[8,4096]{1,0:T(8,128)S(1)} %get-tuple-element.20.mine, f32[8,4096]{1,0:T(8,128)S(1)} %collective-permute-done.mate, f32[4,4096]{1,0:T(4,128)S(1)} %collective-permute-done.1.beside, ...), custom_call_target="tpu_custom_call" | custom-call | tf_op jit(solution)/shard_map/pallas_call | solution.py:296
  11.9 0.2 collective-permute-start.3
  12.1 1.2 %collective-permute-done.3.mate = f32[8,4096]{1,0:T(8,128)S(1)} collective-permute-done((f32[8,4096]{1,0:T(8,128)S(1)}, f32[8,4096]{1,0:T(8,128)S(1)}, u32[]{:S(2)}, u32[]{:S(2)}) %collective-permute-start.3) | collective-permute-done | bytes 131104 | tf_op jit(solution)/shard_map/ppermute | solution.py:326
  13.3 2.1 %collective-permute-start.4 = (f32[4,4096]{1,0:T(4,128)S(1)}, f32[4,4096]{1,0:T(4,128)S(1)}, u32[]{:S(2)}, u32[]{:S(2)}) collective-permute-start(f32[4,4096]{1,0:T(4,128)S(1)} %shard_map.78), channel_id=1, source_target_pairs={{1,2},{3,4},{5,6},{7,8},{9,10},{11,12},{13,14},{17,18},{19,20},{21... | collective-permute-start | bytes 196616 | tf_op jit(solution)/shard_map/ppermute | solution.py:329
  15.4 2.2 %collective-permute-done.4.beside = f32[4,4096]{1,0:T(4,128)S(1)} collective-permute-done((f32[4,4096]{1,0:T(4,128)S(1)}, f32[4,4096]{1,0:T(4,128)S(1)}, u32[]{:S(2)}, u32[]{:S(2)}) %collective-permute-start.4) | collective-permute-done | bytes 65568 | tf_op jit(solution)/shard_map/ppermute | solution.py:329
  17.7 0.1 collective-permute-start.5
  17.8 1.1 %collective-permute-done.5.relayed = f32[4,4096]{1,0:T(4,128)S(1)} collective-permute-done((f32[4,4096]{1,0:T(4,128)S(1)}, f32[4,4096]{1,0:T(4,128)S(1)}, u32[]{:S(2)}, u32[]{:S(2)}) %collective-permute-start.5) | collective-permute-done | bytes 65568 | tf_op jit(solution)/shard_map/ppermute | solution.py:326
  18.9 0.9 %shard_map.79 = (f32[8,4096]{1,0:T(8,128)S(1)}, bf16[64,4096]{1,0:T(8,128)(2,1)S(1)}) custom-call(s32[1]{0:T(128)} %bitcast.slab_ref, f32[8,4096]{1,0:T(8,128)S(1)} %get-tuple-element.26.mine, f32[8,4096]{1,0:T(8,128)S(1)} %collective-permute-done.3.mate, f32[4,4096]{1,0:T(4,128)S(1)} %collective-permute-done.4.beside, ...), custom_call_target="tpu_custom_call" | custom-call | tf_op jit(solution)/shard_map/pallas_call | solution.py:296
  19.8 0.2 collective-permute-start.6
  20.0 1.2 %collective-permute-done.6.mate = f32[8,4096]{1,0:T(8,128)S(1)} collective-permute-done((f32[8,4096]{1,0:T(8,128)S(1)}, f32[8,4096]{1,0:T(8,128)S(1)}, u32[]{:S(2)}, u32[]{:S(2)}) %collective-permute-start.6) | collective-permute-done | bytes 131104 | tf_op jit(solution)/shard_map/ppermute | solution.py:326
  21.2 0.2 collective-permute-start.7
  21.4 2.0 %collective-permute-start.8 = (bf16[64,4096]{1,0:T(8,128)(2,1)S(1)}, bf16[64,4096]{1,0:T(8,128)(2,1)S(1)}, u32[]{:S(2)}, u32[]{:S(2)}) collective-permute-start(bf16[64,4096]{1,0:T(8,128)(2,1)S(1)} %get-tuple-element.30.maps), channel_id=1, source_target_pairs={{1,2},{3,4},{5,6},{7,8},{9,10},{11,12},{13,14},{17,18},{19,20},{21... | collective-permute-start | bytes 1572872 | tf_op jit(solution)/shard_map/ppermute | solution.py:329
  23.5 0.0 collective-permute-start.9
  23.5 7.8 %collective-permute-done.9.beside = f32[4,4096]{1,0:T(4,128)S(1)} collective-permute-done((f32[4,4096]{1,0:T(4,128)S(1)}, f32[4,4096]{1,0:T(4,128)S(1)}, u32[]{:S(2)}, u32[]{:S(2)}) %collective-permute-start.9) | collective-permute-done | bytes 65568 | tf_op jit(solution)/shard_map/ppermute | solution.py:329
  31.3 0.0 collective-permute-done.7.mate_maps
  31.3 1.5 %shard_map.82 = (f32[16,128]{1,0:T(8,128)S(1)}, f32[64,128]{1,0:T(8,128)}) custom-call(s32[1]{0:T(128)} %bitcast.slab_ref, f32[8,4096]{1,0:T(8,128)S(1)} %get-tuple-element.28.mine, f32[8,4096]{1,0:T(8,128)S(1)} %collective-permute-done.6.mate, f32[4,4096]{1,0:T(4,128)S(1)} %collective-permute-done.9.beside, bf16[64,4096]{1,0:T(8,128)(2,1)S(1)} %get-tuple-element.30.maps, ...), custom_call_target="tpu_custom_call" | custom-call | tf_op jit(solution)/shard_map/pallas_call | solution.py:296
  32.8 2.9 %collective-permute-start.10 = (f32[16,128]{1,0:T(8,128)S(1)}, f32[16,128]{1,0:T(8,128)S(1)}, u32[]{:S(2)}, u32[]{:S(2)}) collective-permute-start(f32[16,128]{1,0:T(8,128)S(1)} %get-tuple-element.32.refs_0_), channel_id=1, source_target_pairs={{0,3},{1,2},{2,1},{3,0},{4,7},{5,6},{6,5},{7,4},{8,11},{9,10},{10,... | collective-permute-start | bytes 24584 | tf_op jit(solution)/shard_map/ppermute | solution.py:397
  35.7 5.7 %collective-permute-start.11 = (f32[16,128]{1,0:T(8,128)S(1)}, f32[16,128]{1,0:T(8,128)S(1)}, u32[]{:S(2)}, u32[]{:S(2)}) collective-permute-start(f32[16,128]{1,0:T(8,128)S(1)} %get-tuple-element.32.refs_0_), channel_id=1, source_target_pairs={{0,2},{1,3},{2,0},{3,1},{4,6},{5,7},{6,4},{7,5},{8,10},{9,11},{10,... | collective-permute-start | bytes 24584 | tf_op jit(solution)/shard_map/ppermute | solution.py:397
  41.3 0.1 collective-permute-start.12
  41.4 0.0 collective-permute-done.10.refs_1_
  41.4 1.6 %collective-permute-done.11.refs_2_ = f32[16,128]{1,0:T(8,128)S(1)} collective-permute-done((f32[16,128]{1,0:T(8,128)S(1)}, f32[16,128]{1,0:T(8,128)S(1)}, u32[]{:S(2)}, u32[]{:S(2)}) %collective-permute-start.11) | collective-permute-done | bytes 8224 | tf_op jit(solution)/shard_map/ppermute | solution.py:397
  43.0 0.0 collective-permute-done.12.refs_3_
  43.0 4.3 %collective-permute-start.13 = (f32[16,128]{1,0:T(8,128)S(1)}, f32[16,128]{1,0:T(8,128)S(1)}, u32[]{:S(2)}, u32[]{:S(2)}) collective-permute-start(f32[16,128]{1,0:T(8,128)S(1)} %shard_map.83.rest_0_), channel_id=1, source_target_pairs={{0,12},{1,13},{2,14},{3,15},{4,8},{5,9},{6,10},{7,11},{8,4},{9,5},... | collective-permute-start | bytes 24584 | tf_op jit(solution)/shard_map/ppermute | solution.py:397
  47.4 0.0 collective-permute-start.14
  47.4 0.6 collective-permute-start.15
  48.0 0.0 collective-permute-done.8.beside_maps
  48.0 1.0 %collective-permute-done.13.rest_1_ = f32[16,128]{1,0:T(8,128)S(1)} collective-permute-done((f32[16,128]{1,0:T(8,128)S(1)}, f32[16,128]{1,0:T(8,128)S(1)}, u32[]{:S(2)}, u32[]{:S(2)}) %collective-permute-start.13) | collective-permute-done | bytes 8224 | tf_op jit(solution)/shard_map/ppermute | solution.py:397
  49.0 2.9 %collective-permute-done.14.rest_2_ = f32[16,128]{1,0:T(8,128)S(1)} collective-permute-done((f32[16,128]{1,0:T(8,128)S(1)}, f32[16,128]{1,0:T(8,128)S(1)}, u32[]{:S(2)}, u32[]{:S(2)}) %collective-permute-start.14) | collective-permute-done | bytes 8224 | tf_op jit(solution)/shard_map/ppermute | solution.py:397
  51.9 0.0 collective-permute-done.15.rest_3_
  51.9 2.0 %shard_map.84 = (f32[32,64]{1,0:T(8,128)}, f32[16,128]{1,0:T(8,128)}) custom-call(s32[1]{0:T(128)} %bitcast.slab_ref, bf16[64,4096]{1,0:T(8,128)(2,1)S(1)} %get-tuple-element.30.maps, bf16[64,4096]{1,0:T(8,128)(2,1)S(1)} %collective-permute-done.7.mate_maps, bf16[64,4096]{1,0:T(8,128)(2,1)S(1)} %collective-permute-done.8.beside_maps, ...), custom_call_target="tpu_custom_call" | custom-call | tf_op jit(solution)/shard_map/pallas_call | solution.py:296
  54.0 4.8 %all-to-all-start = ((f32[16,1,128]{2,1,0:T(1,128)}), f32[16,1,128]{2,1,0:T(1,128)S(1)}, u32[]{:S(2)}, u32[]{:S(2)}) async-start(f32[16,1,128]{2,1,0:T(1,128)} %bitcast.6), calls=%async_computation | async-start | bytes 16384 | tf_op jit(solution)/shard_map/all_to_all | solution.py:408
  58.7 1.9 %shard_map.81 = bf16[2048,128]{1,0:T(8,128)(2,1)} custom-call(bf16[64,4096]{1,0:T(8,128)(2,1)S(1)} %get-tuple-element.30.maps), custom_call_target="tpu_custom_call" | custom-call | tf_op jit(solution)/shard_map/pallas_call | solution.py:296
  60.6 4.6 %all-to-all-done = f32[16,1,128]{2,1,0:T(1,128)S(1)} async-done(((f32[16,1,128]{2,1,0:T(1,128)}), f32[16,1,128]{2,1,0:T(1,128)S(1)}, u32[]{:S(2)}, u32[]{:S(2)}) %all-to-all-start) | async-done | bytes 8224 | tf_op jit(solution)/shard_map/all_to_all | solution.py:408
  65.2 0.6 slice_reduce_fusion
  (4 shorter events, 0.1 us)
Async XLA Ops:
  2.8 1.5 %collective-permute-start = (f32[8,4096]{1,0:T(8,128)S(1)}, f32[8,4096]{1,0:T(8,128)S(1)}, u32[]{:S(2)}, u32[]{:S(2)}) collective-permute-start(f32[8,4096]{1,0:T(8,128)S(1)} %get-tuple-element.20.mine), channel_id=1, source_target_pairs={{0,1},{1,0},{2,3},{3,2},{4,5},{5,4},{6,7},{7,6},{8,9},{9,8},{10,11... | collective-permute-start | bytes 393224 | tf_op jit(solution)/shard_map/ppermute | solution.py:326
  4.4 5.1 %collective-permute-start.1 = (f32[4,4096]{1,0:T(4,128)S(1)}, f32[4,4096]{1,0:T(4,128)S(1)}, u32[]{:S(2)}, u32[]{:S(2)}) collective-permute-start(f32[4,4096]{1,0:T(4,128)S(1)} %shard_map.76), channel_id=1, source_target_pairs={{1,2},{3,4},{5,6},{7,8},{9,10},{11,12},{13,14},{17,18},{19,20},{21... | collective-permute-start | bytes 196616 | tf_op jit(solution)/shard_map/ppermute | solution.py:329
  9.6 1.3 %collective-permute-start.2 = (f32[4,4096]{1,0:T(4,128)S(1)}, f32[4,4096]{1,0:T(4,128)S(1)}, u32[]{:S(2)}, u32[]{:S(2)}) collective-permute-start(f32[4,4096]{1,0:T(4,128)S(1)} %collective-permute-done.1.beside), channel_id=1, source_target_pairs={{0,1},{1,0},{2,3},{3,2},{4,5},{5,4},{6,7},{7,6},{8,9},{9,8},{10,11... | collective-permute-start | bytes 196616 | tf_op jit(solution)/shard_map/ppermute | solution.py:326
  11.9 1.4 %collective-permute-start.3 = (f32[8,4096]{1,0:T(8,128)S(1)}, f32[8,4096]{1,0:T(8,128)S(1)}, u32[]{:S(2)}, u32[]{:S(2)}) collective-permute-start(f32[8,4096]{1,0:T(8,128)S(1)} %get-tuple-element.26.mine), channel_id=1, source_target_pairs={{0,1},{1,0},{2,3},{3,2},{4,5},{5,4},{6,7},{7,6},{8,9},{9,8},{10,11... | collective-permute-start | bytes 393224 | tf_op jit(solution)/shard_map/ppermute | solution.py:326
  13.3 4.3 %collective-permute-start.4 = (f32[4,4096]{1,0:T(4,128)S(1)}, f32[4,4096]{1,0:T(4,128)S(1)}, u32[]{:S(2)}, u32[]{:S(2)}) collective-permute-start(f32[4,4096]{1,0:T(4,128)S(1)} %shard_map.78), channel_id=1, source_target_pairs={{1,2},{3,4},{5,6},{7,8},{9,10},{11,12},{13,14},{17,18},{19,20},{21... | collective-permute-start | bytes 196616 | tf_op jit(solution)/shard_map/ppermute | solution.py:329
  17.7 1.3 %collective-permute-start.5 = (f32[4,4096]{1,0:T(4,128)S(1)}, f32[4,4096]{1,0:T(4,128)S(1)}, u32[]{:S(2)}, u32[]{:S(2)}) collective-permute-start(f32[4,4096]{1,0:T(4,128)S(1)} %collective-permute-done.4.beside), channel_id=1, source_target_pairs={{0,1},{1,0},{2,3},{3,2},{4,5},{5,4},{6,7},{7,6},{8,9},{9,8},{10,11... | collective-permute-start | bytes 196616 | tf_op jit(solution)/shard_map/ppermute | solution.py:326
  19.8 1.4 %collective-permute-start.6 = (f32[8,4096]{1,0:T(8,128)S(1)}, f32[8,4096]{1,0:T(8,128)S(1)}, u32[]{:S(2)}, u32[]{:S(2)}) collective-permute-start(f32[8,4096]{1,0:T(8,128)S(1)} %get-tuple-element.28.mine), channel_id=1, source_target_pairs={{0,1},{1,0},{2,3},{3,2},{4,5},{5,4},{6,7},{7,6},{8,9},{9,8},{10,11... | collective-permute-start | bytes 393224 | tf_op jit(solution)/shard_map/ppermute | solution.py:326
  21.2 10.1 %collective-permute-start.7 = (bf16[64,4096]{1,0:T(8,128)(2,1)S(1)}, bf16[64,4096]{1,0:T(8,128)(2,1)S(1)}, u32[]{:S(2)}, u32[]{:S(2)}) collective-permute-start(bf16[64,4096]{1,0:T(8,128)(2,1)S(1)} %get-tuple-element.30.maps), channel_id=1, source_target_pairs={{0,1},{1,0},{2,3},{3,2},{4,5},{5,4},{6,7},{7,6},{8,9},{9,8},{10,11... | collective-permute-start | bytes 1572872 | tf_op jit(solution)/shard_map/ppermute | solution.py:326
  21.4 26.6 %collective-permute-start.8 = (bf16[64,4096]{1,0:T(8,128)(2,1)S(1)}, bf16[64,4096]{1,0:T(8,128)(2,1)S(1)}, u32[]{:S(2)}, u32[]{:S(2)}) collective-permute-start(bf16[64,4096]{1,0:T(8,128)(2,1)S(1)} %get-tuple-element.30.maps), channel_id=1, source_target_pairs={{1,2},{3,4},{5,6},{7,8},{9,10},{11,12},{13,14},{17,18},{19,20},{21... | collective-permute-start | bytes 1572872 | tf_op jit(solution)/shard_map/ppermute | solution.py:329
  23.5 7.9 %collective-permute-start.9 = (f32[4,4096]{1,0:T(4,128)S(1)}, f32[4,4096]{1,0:T(4,128)S(1)}, u32[]{:S(2)}, u32[]{:S(2)}) collective-permute-start(f32[4,4096]{1,0:T(4,128)S(1)} %shard_map.80), channel_id=1, source_target_pairs={{1,2},{3,4},{5,6},{7,8},{9,10},{11,12},{13,14},{17,18},{19,20},{21... | collective-permute-start | bytes 196616 | tf_op jit(solution)/shard_map/ppermute | solution.py:329
  32.8 8.6 %collective-permute-start.10 = (f32[16,128]{1,0:T(8,128)S(1)}, f32[16,128]{1,0:T(8,128)S(1)}, u32[]{:S(2)}, u32[]{:S(2)}) collective-permute-start(f32[16,128]{1,0:T(8,128)S(1)} %get-tuple-element.32.refs_0_), channel_id=1, source_target_pairs={{0,3},{1,2},{2,1},{3,0},{4,7},{5,6},{6,5},{7,4},{8,11},{9,10},{10,... | collective-permute-start | bytes 24584 | tf_op jit(solution)/shard_map/ppermute | solution.py:397
  35.7 7.4 %collective-permute-start.11 = (f32[16,128]{1,0:T(8,128)S(1)}, f32[16,128]{1,0:T(8,128)S(1)}, u32[]{:S(2)}, u32[]{:S(2)}) collective-permute-start(f32[16,128]{1,0:T(8,128)S(1)} %get-tuple-element.32.refs_0_), channel_id=1, source_target_pairs={{0,2},{1,3},{2,0},{3,1},{4,6},{5,7},{6,4},{7,5},{8,10},{9,11},{10,... | collective-permute-start | bytes 24584 | tf_op jit(solution)/shard_map/ppermute | solution.py:397
  41.3 1.7 %collective-permute-start.12 = (f32[16,128]{1,0:T(8,128)S(1)}, f32[16,128]{1,0:T(8,128)S(1)}, u32[]{:S(2)}, u32[]{:S(2)}) collective-permute-start(f32[16,128]{1,0:T(8,128)S(1)} %get-tuple-element.32.refs_0_), channel_id=1, source_target_pairs={{0,1},{1,0},{2,3},{3,2},{4,5},{5,4},{6,7},{7,6},{8,9},{9,8},{10,11... | collective-permute-start | bytes 24584 | tf_op jit(solution)/shard_map/ppermute | solution.py:397
  43.0 6.0 %collective-permute-start.13 = (f32[16,128]{1,0:T(8,128)S(1)}, f32[16,128]{1,0:T(8,128)S(1)}, u32[]{:S(2)}, u32[]{:S(2)}) collective-permute-start(f32[16,128]{1,0:T(8,128)S(1)} %shard_map.83.rest_0_), channel_id=1, source_target_pairs={{0,12},{1,13},{2,14},{3,15},{4,8},{5,9},{6,10},{7,11},{8,4},{9,5},... | collective-permute-start | bytes 24584 | tf_op jit(solution)/shard_map/ppermute | solution.py:397
  47.4 4.5 %collective-permute-start.14 = (f32[16,128]{1,0:T(8,128)S(1)}, f32[16,128]{1,0:T(8,128)S(1)}, u32[]{:S(2)}, u32[]{:S(2)}) collective-permute-start(f32[16,128]{1,0:T(8,128)S(1)} %shard_map.83.rest_0_), channel_id=1, source_target_pairs={{0,8},{1,9},{2,10},{3,11},{4,12},{5,13},{6,14},{7,15},{8,0},{9,1},... | collective-permute-start | bytes 24584 | tf_op jit(solution)/shard_map/ppermute | solution.py:397
  47.4 4.5 %collective-permute-start.15 = (f32[16,128]{1,0:T(8,128)S(1)}, f32[16,128]{1,0:T(8,128)S(1)}, u32[]{:S(2)}, u32[]{:S(2)}) collective-permute-start(f32[16,128]{1,0:T(8,128)S(1)} %shard_map.83.rest_0_), channel_id=1, source_target_pairs={{0,4},{1,5},{2,6},{3,7},{4,0},{5,1},{6,2},{7,3},{8,12},{9,13},{10,... | collective-permute-start | bytes 24584 | tf_op jit(solution)/shard_map/ppermute | solution.py:397
  54.0 11.2 %all-to-all-start = ((f32[16,1,128]{2,1,0:T(1,128)}), f32[16,1,128]{2,1,0:T(1,128)S(1)}, u32[]{:S(2)}, u32[]{:S(2)}) async-start(f32[16,1,128]{2,1,0:T(1,128)} %bitcast.6), calls=%async_computation | async-start | bytes 16384 | tf_op jit(solution)/shard_map/all_to_all | solution.py:408

commit v5 on v4

--- a/solution.py
+++ b/solution.py
@@ -328,6 +328,20 @@
     def to_beside(x):
         return lax.ppermute(x, ("vol", "gz"), besides)
 
+    def everywhere(x, strides):
+        terms = [x]
+        for stride in strides:
+            if len(terms) > 1:
+                terms = call(sum_kernel, [(x.shape, F32)], terms, (), [pltpu.VMEM] * len(terms))
+            terms = list(terms)
+            for k in (3, 2, 1):
+                if k * stride < slabs:
+                    swaps = [(i, i ^ (k * stride)) for i in range(slabs)]
+                    terms.append(lax.ppermute(terms[0], "gz", swaps))
+        return terms
+
+    strides = [4**k for k in range(slabs.bit_length()) if 4**k < slabs]
+
     share_shape = ((8, size), F32)
     maps_shape = ((2 * atom_count, size), BF16)
     natural_shape = (natural.shape, BF16)
@@ -388,25 +402,15 @@
         (slab, mine, mate, beside, maps, mate_maps),
         [unfolded, ((8 * height, breadth), F32)],
     )
-    shares = [packed]
-    stride = 1
-    while stride < slabs:
-        if len(shares) > 1:
-            shares = call(sum_kernel, [packed_shape], shares, (), [pltpu.VMEM] * len(shares))
-        shares = [*shares] + [
-            lax.ppermute(shares[0], "gz", [(i, i ^ (k * stride)) for i in range(slabs)])
-            for k in (3, 2, 1)
-            if k * stride < slabs
-        ]
-        stride *= 4
+    shares = everywhere(packed, strides[::-1])
     descent, norms = call(
         functools.partial(probe_kernel, height, breadth, slabs),
-        [((atom_count, 64), F32), ((slabs, 128), F32)],
+        [((atom_count, 64), F32), ((8, 128), F32)],
         (slab, maps, mate_maps, beside_maps, *shares),
         [products, ((8, breadth), F32)],
     )
-    norms = lax.all_to_all(norms.reshape(slabs, 1, 128), "gz", 0, 0)
-    curvature = jnp.sum(norms[:, :, :1]).reshape(1)
+    norms = everywhere(norms, strides)
+    curvature = sum(norms[1:], norms[0])[0, :1]
     return (
         natural.reshape(initial_maps.shape),
         descent,

time: 66 us -> 64 us (0.970)
  waiting for transfers between devices: 28 us -> 26 us
    ppermute x6 -> x12, starting transfers between devices: 13.6 us -> 18.7 us  [everywhere(): terms.append(lax.ppermute(terms[0], 'gz', swaps))]
    all_to_all x1 -> x0, starting transfers between devices: 4.78 us -> none  [per_device(): norms = lax.all_to_all(norms.reshape(slabs, 1, 128), 'gz', 0, 0)]
    all_to_all x1 -> x0, waiting for transfers between devices: 4.55 us -> none  [per_device(): norms = lax.all_to_all(norms.reshape(slabs, 1, 128), 'gz', 0, 0)]
    ppermute x6 -> x12, waiting for transfers between devices: 5.5 us -> 7.97 us  [everywhere(): terms.append(lax.ppermute(terms[0], 'gz', swaps))]
    pallas_call x10 -> x11, Pallas kernels: 9.56 us -> 9.43 us  [call(): pl.pallas_call(kernel, out_shape=[jax.ShapeDtypeStruct(shape, dtype) for...]
  transfers between devices with their start and end apart: 17 -> 22, of which waited for: 12 -> 14; matrix products, arithmetic and copies ran while one was open for 0% -> 0% of each run, Pallas kernels for 5% -> 5%
where the time goes in v5:
time: 64 us; the launch traced here: 63.8 us
  starting transfers between devices  27.2 us (42%)
  waiting for transfers between devices  26 us (41%)
  Pallas kernels  9.43 us (15%)
  between operations  0.7 us (1%)
    ppermute x12, starting transfers between devices, everywhere(): terms.append(lax.ppermute(terms[0], 'gz', swaps))  18.7 us
    ppermute x4, waiting for transfers between devices, to_beside(): return lax.ppermute(x, ('vol', 'gz'), besides)  12.3 us
    pallas_call x11, Pallas kernels, call(): pl.pallas_call(kernel, out_shape=[jax.ShapeDtypeStruct(shape, dtype) for...  9.43 us
    ppermute x12, waiting for transfers between devices, everywhere(): terms.append(lax.ppermute(terms[0], 'gz', swaps))  7.97 us
    ppermute x4, starting transfers between devices, to_beside(): return lax.ppermute(x, ('vol', 'gz'), besides)  7.02 us
    ppermute x6, waiting for transfers between devices, to_mate(): return lax.ppermute(x, 'gz', mates)  5.64 us
    ppermute x6, starting transfers between devices, to_mate(): return lax.ppermute(x, 'gz', mates)  1.47 us
  transfers between devices with their start and end apart: 22, of which 14 were waited for; matrix products, arithmetic and copies ran while one was open for 0% of the time, Pallas kernels for 5%

profile of v5, /device:TPU:0, one launch (start us, length us, event | category | flops | bytes accessed | tf_op | source)
XLA Modules:
  0.0 63.8 jit_solution(12154624111069377684)
XLA Ops:
  0.6 2.2 %shard_map.75 = (f32[8,4096]{1,0:T(8,128)S(1)}, bf16[64,4096]{1,0:T(8,128)(2,1)S(1)}, bf16[64,128]{1,0:T(8,128)(2,1)S(1)}, bf16[128,64]{1,0:T(8,128)(2,1)S(1)}, ...) custom-call(s32[1]{0:T(128)} %bitcast.slab_ref, bf16[2048,128]{1,0:T(8,128)(2,1)} %bitcast.7, f32[64,128]{1,0:T(8,128)} %bitcast.9, ...), custom_call_target="tpu_custom_call" | custom-call | tf_op jit(solution)/shard_map/pallas_call | solution.py:296
  2.8 0.6 collective-permute-start
  3.4 1.0 %collective-permute-done.mate = f32[8,4096]{1,0:T(8,128)S(1)} collective-permute-done((f32[8,4096]{1,0:T(8,128)S(1)}, f32[8,4096]{1,0:T(8,128)S(1)}, u32[]{:S(2)}, u32[]{:S(2)}) %collective-permute-start) | collective-permute-done | bytes 131104 | tf_op jit(solution)/shard_map/ppermute | solution.py:326
  4.4 2.9 %collective-permute-start.1 = (f32[4,4096]{1,0:T(4,128)S(1)}, f32[4,4096]{1,0:T(4,128)S(1)}, u32[]{:S(2)}, u32[]{:S(2)}) collective-permute-start(f32[4,4096]{1,0:T(4,128)S(1)} %shard_map.76), channel_id=1, source_target_pairs={{1,2},{3,4},{5,6},{7,8},{9,10},{11,12},{13,14},{17,18},{19,20},{21... | collective-permute-start | bytes 196616 | tf_op jit(solution)/shard_map/ppermute | solution.py:329
  7.3 2.2 %collective-permute-done.1.beside = f32[4,4096]{1,0:T(4,128)S(1)} collective-permute-done((f32[4,4096]{1,0:T(4,128)S(1)}, f32[4,4096]{1,0:T(4,128)S(1)}, u32[]{:S(2)}, u32[]{:S(2)}) %collective-permute-start.1) | collective-permute-done | bytes 65568 | tf_op jit(solution)/shard_map/ppermute | solution.py:329
  9.6 0.1 collective-permute-start.2
  9.7 1.1 %collective-permute-done.2.relayed = f32[4,4096]{1,0:T(4,128)S(1)} collective-permute-done((f32[4,4096]{1,0:T(4,128)S(1)}, f32[4,4096]{1,0:T(4,128)S(1)}, u32[]{:S(2)}, u32[]{:S(2)}) %collective-permute-start.2) | collective-permute-done | bytes 65568 | tf_op jit(solution)/shard_map/ppermute | solution.py:326
  10.8 1.1 %shard_map.77 = (f32[8,4096]{1,0:T(8,128)S(1)}, bf16[64,4096]{1,0:T(8,128)(2,1)S(1)}) custom-call(s32[1]{0:T(128)} %bitcast.slab_ref, f32[8,4096]{1,0:T(8,128)S(1)} %get-tuple-element.20.mine, f32[8,4096]{1,0:T(8,128)S(1)} %collective-permute-done.mate, f32[4,4096]{1,0:T(4,128)S(1)} %collective-permute-done.1.beside, ...), custom_call_target="tpu_custom_call" | custom-call | tf_op jit(solution)/shard_map/pallas_call | solution.py:296
  11.9 0.2 collective-permute-start.3
  12.1 1.2 %collective-permute-done.3.mate = f32[8,4096]{1,0:T(8,128)S(1)} collective-permute-done((f32[8,4096]{1,0:T(8,128)S(1)}, f32[8,4096]{1,0:T(8,128)S(1)}, u32[]{:S(2)}, u32[]{:S(2)}) %collective-permute-start.3) | collective-permute-done | bytes 131104 | tf_op jit(solution)/shard_map/ppermute | solution.py:326
  13.3 2.1 %collective-permute-start.4 = (f32[4,4096]{1,0:T(4,128)S(1)}, f32[4,4096]{1,0:T(4,128)S(1)}, u32[]{:S(2)}, u32[]{:S(2)}) collective-permute-start(f32[4,4096]{1,0:T(4,128)S(1)} %shard_map.78), channel_id=1, source_target_pairs={{1,2},{3,4},{5,6},{7,8},{9,10},{11,12},{13,14},{17,18},{19,20},{21... | collective-permute-start | bytes 196616 | tf_op jit(solution)/shard_map/ppermute | solution.py:329
  15.4 2.2 %collective-permute-done.4.beside = f32[4,4096]{1,0:T(4,128)S(1)} collective-permute-done((f32[4,4096]{1,0:T(4,128)S(1)}, f32[4,4096]{1,0:T(4,128)S(1)}, u32[]{:S(2)}, u32[]{:S(2)}) %collective-permute-start.4) | collective-permute-done | bytes 65568 | tf_op jit(solution)/shard_map/ppermute | solution.py:329
  17.7 0.1 collective-permute-start.5
  17.8 1.1 %collective-permute-done.5.relayed = f32[4,4096]{1,0:T(4,128)S(1)} collective-permute-done((f32[4,4096]{1,0:T(4,128)S(1)}, f32[4,4096]{1,0:T(4,128)S(1)}, u32[]{:S(2)}, u32[]{:S(2)}) %collective-permute-start.5) | collective-permute-done | bytes 65568 | tf_op jit(solution)/shard_map/ppermute | solution.py:326
  18.9 0.9 %shard_map.79 = (f32[8,4096]{1,0:T(8,128)S(1)}, bf16[64,4096]{1,0:T(8,128)(2,1)S(1)}) custom-call(s32[1]{0:T(128)} %bitcast.slab_ref, f32[8,4096]{1,0:T(8,128)S(1)} %get-tuple-element.26.mine, f32[8,4096]{1,0:T(8,128)S(1)} %collective-permute-done.3.mate, f32[4,4096]{1,0:T(4,128)S(1)} %collective-permute-done.4.beside, ...), custom_call_target="tpu_custom_call" | custom-call | tf_op jit(solution)/shard_map/pallas_call | solution.py:296
  19.8 0.2 collective-permute-start.6
  20.0 1.2 %collective-permute-done.6.mate = f32[8,4096]{1,0:T(8,128)S(1)} collective-permute-done((f32[8,4096]{1,0:T(8,128)S(1)}, f32[8,4096]{1,0:T(8,128)S(1)}, u32[]{:S(2)}, u32[]{:S(2)}) %collective-permute-start.6) | collective-permute-done | bytes 131104 | tf_op jit(solution)/shard_map/ppermute | solution.py:326
  21.2 0.2 collective-permute-start.7
  21.4 2.0 %collective-permute-start.8 = (bf16[64,4096]{1,0:T(8,128)(2,1)S(1)}, bf16[64,4096]{1,0:T(8,128)(2,1)S(1)}, u32[]{:S(2)}, u32[]{:S(2)}) collective-permute-start(bf16[64,4096]{1,0:T(8,128)(2,1)S(1)} %get-tuple-element.30.maps), channel_id=1, source_target_pairs={{1,2},{3,4},{5,6},{7,8},{9,10},{11,12},{13,14},{17,18},{19,20},{21... | collective-permute-start | bytes 1572872 | tf_op jit(solution)/shard_map/ppermute | solution.py:329
  23.5 0.0 collective-permute-start.9
  23.5 7.8 %collective-permute-done.9.beside = f32[4,4096]{1,0:T(4,128)S(1)} collective-permute-done((f32[4,4096]{1,0:T(4,128)S(1)}, f32[4,4096]{1,0:T(4,128)S(1)}, u32[]{:S(2)}, u32[]{:S(2)}) %collective-permute-start.9) | collective-permute-done | bytes 65568 | tf_op jit(solution)/shard_map/ppermute | solution.py:329
  31.3 0.0 collective-permute-done.7.mate_maps
  31.3 1.5 %shard_map.82 = (f32[16,128]{1,0:T(8,128)S(1)}, f32[64,128]{1,0:T(8,128)}) custom-call(s32[1]{0:T(128)} %bitcast.slab_ref, f32[8,4096]{1,0:T(8,128)S(1)} %get-tuple-element.28.mine, f32[8,4096]{1,0:T(8,128)S(1)} %collective-permute-done.6.mate, f32[4,4096]{1,0:T(4,128)S(1)} %collective-permute-done.9.beside, bf16[64,4096]{1,0:T(8,128)(2,1)S(1)} %get-tuple-element.30.maps, ...), custom_call_target="tpu_custom_call" | custom-call | tf_op jit(solution)/shard_map/pallas_call | solution.py:296
  32.8 5.4 %collective-permute-start.10 = (f32[16,128]{1,0:T(8,128)S(1)}, f32[16,128]{1,0:T(8,128)S(1)}, u32[]{:S(2)}, u32[]{:S(2)}) collective-permute-start(f32[16,128]{1,0:T(8,128)S(1)} %get-tuple-element.32.refs_0_), channel_id=1, source_target_pairs={{0,12},{1,13},{2,14},{3,15},{4,8},{5,9},{6,10},{7,11},{8,4},{9,5},... | collective-permute-start | bytes 24584 | tf_op jit(solution)/shard_map/ppermute | solution.py:340
  38.2 0.0 collective-permute-start.11
  38.2 0.6 collective-permute-start.12
  38.8 1.1 %collective-permute-done.10.refs_1_ = f32[16,128]{1,0:T(8,128)S(1)} collective-permute-done((f32[16,128]{1,0:T(8,128)S(1)}, f32[16,128]{1,0:T(8,128)S(1)}, u32[]{:S(2)}, u32[]{:S(2)}) %collective-permute-start.10) | collective-permute-done | bytes 8224 | tf_op jit(solution)/shard_map/ppermute | solution.py:340
  39.8 2.9 %collective-permute-done.11.refs_2_ = f32[16,128]{1,0:T(8,128)S(1)} collective-permute-done((f32[16,128]{1,0:T(8,128)S(1)}, f32[16,128]{1,0:T(8,128)S(1)}, u32[]{:S(2)}, u32[]{:S(2)}) %collective-permute-start.11) | collective-permute-done | bytes 8224 | tf_op jit(solution)/shard_map/ppermute | solution.py:340
  42.8 0.0 collective-permute-done.12.refs_3_
  42.8 0.1 collective-permute-start.13
  42.9 6.2 %collective-permute-start.14 = (f32[16,128]{1,0:T(8,128)S(1)}, f32[16,128]{1,0:T(8,128)S(1)}, u32[]{:S(2)}, u32[]{:S(2)}) collective-permute-start(f32[16,128]{1,0:T(8,128)S(1)} %shard_map.83.rest_0_), channel_id=1, source_target_pairs={{0,2},{1,3},{2,0},{3,1},{4,6},{5,7},{6,4},{7,5},{8,10},{9,11},{10,... | collective-permute-start | bytes 24584 | tf_op jit(solution)/shard_map/ppermute | solution.py:340
  49.0 0.0 collective-permute-start.15
  49.0 0.0 collective-permute-done.8.beside_maps
  49.0 0.0 collective-permute-done.13.rest_1_
  49.0 1.7 %collective-permute-done.14.rest_2_ = f32[16,128]{1,0:T(8,128)S(1)} collective-permute-done((f32[16,128]{1,0:T(8,128)S(1)}, f32[16,128]{1,0:T(8,128)S(1)}, u32[]{:S(2)}, u32[]{:S(2)}) %collective-permute-start.14) | collective-permute-done | bytes 8224 | tf_op jit(solution)/shard_map/ppermute | solution.py:340
  50.7 1.9 %shard_map.84 = (f32[32,64]{1,0:T(8,128)}, f32[8,128]{1,0:T(8,128)S(1)}) custom-call(s32[1]{0:T(128)} %bitcast.slab_ref, bf16[64,4096]{1,0:T(8,128)(2,1)S(1)} %get-tuple-element.30.maps, bf16[64,4096]{1,0:T(8,128)(2,1)S(1)} %collective-permute-done.7.mate_maps, bf16[64,4096]{1,0:T(8,128)(2,1)S(1)} %collective-permute-done.8.beside_maps, ...), custom_call_target="tpu_custom_call" | custom-call | tf_op jit(solution)/shard_map/pallas_call | solution.py:296
  52.6 0.3 collective-permute-start.16
  52.9 1.6 %collective-permute-start.17 = (f32[8,128]{1,0:T(8,128)S(1)}, f32[8,128]{1,0:T(8,128)S(1)}, u32[]{:S(2)}, u32[]{:S(2)}) collective-permute-start(f32[8,128]{1,0:T(8,128)S(1)} %get-tuple-element.34.refs_0_), channel_id=1, source_target_pairs={{0,2},{1,3},{2,0},{3,1},{4,6},{5,7},{6,4},{7,5},{8,10},{9,11},{10,... | collective-permute-start | bytes 12296 | tf_op jit(solution)/shard_map/ppermute | solution.py:340
  54.6 0.1 collective-permute-start.18
  54.7 1.0 %collective-permute-done.16.refs_1_ = f32[8,128]{1,0:T(8,128)S(1)} collective-permute-done((f32[8,128]{1,0:T(8,128)S(1)}, f32[8,128]{1,0:T(8,128)S(1)}, u32[]{:S(2)}, u32[]{:S(2)}) %collective-permute-start.16) | collective-permute-done | bytes 4128 | tf_op jit(solution)/shard_map/ppermute | solution.py:340
  55.6 0.9 %collective-permute-done.17.refs_2_ = f32[8,128]{1,0:T(8,128)S(1)} collective-permute-done((f32[8,128]{1,0:T(8,128)S(1)}, f32[8,128]{1,0:T(8,128)S(1)}, u32[]{:S(2)}, u32[]{:S(2)}) %collective-permute-start.17) | collective-permute-done | bytes 4128 | tf_op jit(solution)/shard_map/ppermute | solution.py:340
  56.5 2.2 %collective-permute-start.19 = (f32[8,128]{1,0:T(8,128)S(1)}, f32[8,128]{1,0:T(8,128)S(1)}, u32[]{:S(2)}, u32[]{:S(2)}) collective-permute-start(f32[8,128]{1,0:T(8,128)S(1)} %shard_map.85), channel_id=1, source_target_pairs={{0,12},{1,13},{2,14},{3,15},{4,8},{5,9},{6,10},{7,11},{8,4},{9,5},... | collective-permute-start | bytes 12296 | tf_op jit(solution)/shard_map/ppermute | solution.py:340
  58.8 0.3 collective-permute-start.20
  59.1 1.9 %collective-permute-start.21 = (f32[8,128]{1,0:T(8,128)S(1)}, f32[8,128]{1,0:T(8,128)S(1)}, u32[]{:S(2)}, u32[]{:S(2)}) collective-permute-start(f32[8,128]{1,0:T(8,128)S(1)} %shard_map.85), channel_id=1, source_target_pairs={{0,4},{1,5},{2,6},{3,7},{4,0},{5,1},{6,2},{7,3},{8,12},{9,13},{10,... | collective-permute-start | bytes 12296 | tf_op jit(solution)/shard_map/ppermute | solution.py:340
  61.0 1.9 %shard_map.81 = bf16[2048,128]{1,0:T(8,128)(2,1)} custom-call(bf16[64,4096]{1,0:T(8,128)(2,1)S(1)} %get-tuple-element.30.maps), custom_call_target="tpu_custom_call" | custom-call | tf_op jit(solution)/shard_map/pallas_call | solution.py:296
  62.9 0.0 collective-permute-done.19
  62.9 0.4 collective-permute-done.20
  63.3 0.5 slice.3
  (9 shorter events, 0.1 us)
Async XLA Ops:
  2.8 1.5 %collective-permute-start = (f32[8,4096]{1,0:T(8,128)S(1)}, f32[8,4096]{1,0:T(8,128)S(1)}, u32[]{:S(2)}, u32[]{:S(2)}) collective-permute-start(f32[8,4096]{1,0:T(8,128)S(1)} %get-tuple-element.20.mine), channel_id=1, source_target_pairs={{0,1},{1,0},{2,3},{3,2},{4,5},{5,4},{6,7},{7,6},{8,9},{9,8},{10,11... | collective-permute-start | bytes 393224 | tf_op jit(solution)/shard_map/ppermute | solution.py:326
  4.4 5.1 %collective-permute-start.1 = (f32[4,4096]{1,0:T(4,128)S(1)}, f32[4,4096]{1,0:T(4,128)S(1)}, u32[]{:S(2)}, u32[]{:S(2)}) collective-permute-start(f32[4,4096]{1,0:T(4,128)S(1)} %shard_map.76), channel_id=1, source_target_pairs={{1,2},{3,4},{5,6},{7,8},{9,10},{11,12},{13,14},{17,18},{19,20},{21... | collective-permute-start | bytes 196616 | tf_op jit(solution)/shard_map/ppermute | solution.py:329
  9.6 1.3 %collective-permute-start.2 = (f32[4,4096]{1,0:T(4,128)S(1)}, f32[4,4096]{1,0:T(4,128)S(1)}, u32[]{:S(2)}, u32[]{:S(2)}) collective-permute-start(f32[4,4096]{1,0:T(4,128)S(1)} %collective-permute-done.1.beside), channel_id=1, source_target_pairs={{0,1},{1,0},{2,3},{3,2},{4,5},{5,4},{6,7},{7,6},{8,9},{9,8},{10,11... | collective-permute-start | bytes 196616 | tf_op jit(solution)/shard_map/ppermute | solution.py:326
  11.9 1.4 %collective-permute-start.3 = (f32[8,4096]{1,0:T(8,128)S(1)}, f32[8,4096]{1,0:T(8,128)S(1)}, u32[]{:S(2)}, u32[]{:S(2)}) collective-permute-start(f32[8,4096]{1,0:T(8,128)S(1)} %get-tuple-element.26.mine), channel_id=1, source_target_pairs={{0,1},{1,0},{2,3},{3,2},{4,5},{5,4},{6,7},{7,6},{8,9},{9,8},{10,11... | collective-permute-start | bytes 393224 | tf_op jit(solution)/shard_map/ppermute | solution.py:326
  13.3 4.3 %collective-permute-start.4 = (f32[4,4096]{1,0:T(4,128)S(1)}, f32[4,4096]{1,0:T(4,128)S(1)}, u32[]{:S(2)}, u32[]{:S(2)}) collective-permute-start(f32[4,4096]{1,0:T(4,128)S(1)} %shard_map.78), channel_id=1, source_target_pairs={{1,2},{3,4},{5,6},{7,8},{9,10},{11,12},{13,14},{17,18},{19,20},{21... | collective-permute-start | bytes 196616 | tf_op jit(solution)/shard_map/ppermute | solution.py:329
  17.7 1.3 %collective-permute-start.5 = (f32[4,4096]{1,0:T(4,128)S(1)}, f32[4,4096]{1,0:T(4,128)S(1)}, u32[]{:S(2)}, u32[]{:S(2)}) collective-permute-start(f32[4,4096]{1,0:T(4,128)S(1)} %collective-permute-done.4.beside), channel_id=1, source_target_pairs={{0,1},{1,0},{2,3},{3,2},{4,5},{5,4},{6,7},{7,6},{8,9},{9,8},{10,11... | collective-permute-start | bytes 196616 | tf_op jit(solution)/shard_map/ppermute | solution.py:326
  19.8 1.4 %collective-permute-start.6 = (f32[8,4096]{1,0:T(8,128)S(1)}, f32[8,4096]{1,0:T(8,128)S(1)}, u32[]{:S(2)}, u32[]{:S(2)}) collective-permute-start(f32[8,4096]{1,0:T(8,128)S(1)} %get-tuple-element.28.mine), channel_id=1, source_target_pairs={{0,1},{1,0},{2,3},{3,2},{4,5},{5,4},{6,7},{7,6},{8,9},{9,8},{10,11... | collective-permute-start | bytes 393224 | tf_op jit(solution)/shard_map/ppermute | solution.py:326
  21.2 10.1 %collective-permute-start.7 = (bf16[64,4096]{1,0:T(8,128)(2,1)S(1)}, bf16[64,4096]{1,0:T(8,128)(2,1)S(1)}, u32[]{:S(2)}, u32[]{:S(2)}) collective-permute-start(bf16[64,4096]{1,0:T(8,128)(2,1)S(1)} %get-tuple-element.30.maps), channel_id=1, source_target_pairs={{0,1},{1,0},{2,3},{3,2},{4,5},{5,4},{6,7},{7,6},{8,9},{9,8},{10,11... | collective-permute-start | bytes 1572872 | tf_op jit(solution)/shard_map/ppermute | solution.py:326
  21.4 27.6 %collective-permute-start.8 = (bf16[64,4096]{1,0:T(8,128)(2,1)S(1)}, bf16[64,4096]{1,0:T(8,128)(2,1)S(1)}, u32[]{:S(2)}, u32[]{:S(2)}) collective-permute-start(bf16[64,4096]{1,0:T(8,128)(2,1)S(1)} %get-tuple-element.30.maps), channel_id=1, source_target_pairs={{1,2},{3,4},{5,6},{7,8},{9,10},{11,12},{13,14},{17,18},{19,20},{21... | collective-permute-start | bytes 1572872 | tf_op jit(solution)/shard_map/ppermute | solution.py:329
  23.5 7.9 %collective-permute-start.9 = (f32[4,4096]{1,0:T(4,128)S(1)}, f32[4,4096]{1,0:T(4,128)S(1)}, u32[]{:S(2)}, u32[]{:S(2)}) collective-permute-start(f32[4,4096]{1,0:T(4,128)S(1)} %shard_map.80), channel_id=1, source_target_pairs={{1,2},{3,4},{5,6},{7,8},{9,10},{11,12},{13,14},{17,18},{19,20},{21... | collective-permute-start | bytes 196616 | tf_op jit(solution)/shard_map/ppermute | solution.py:329
  32.8 7.0 %collective-permute-start.10 = (f32[16,128]{1,0:T(8,128)S(1)}, f32[16,128]{1,0:T(8,128)S(1)}, u32[]{:S(2)}, u32[]{:S(2)}) collective-permute-start(f32[16,128]{1,0:T(8,128)S(1)} %get-tuple-element.32.refs_0_), channel_id=1, source_target_pairs={{0,12},{1,13},{2,14},{3,15},{4,8},{5,9},{6,10},{7,11},{8,4},{9,5},... | collective-permute-start | bytes 24584 | tf_op jit(solution)/shard_map/ppermute | solution.py:340
  38.2 4.5 %collective-permute-start.11 = (f32[16,128]{1,0:T(8,128)S(1)}, f32[16,128]{1,0:T(8,128)S(1)}, u32[]{:S(2)}, u32[]{:S(2)}) collective-permute-start(f32[16,128]{1,0:T(8,128)S(1)} %get-tuple-element.32.refs_0_), channel_id=1, source_target_pairs={{0,8},{1,9},{2,10},{3,11},{4,12},{5,13},{6,14},{7,15},{8,0},{9,1},... | collective-permute-start | bytes 24584 | tf_op jit(solution)/shard_map/ppermute | solution.py:340
  38.2 4.5 %collective-permute-start.12 = (f32[16,128]{1,0:T(8,128)S(1)}, f32[16,128]{1,0:T(8,128)S(1)}, u32[]{:S(2)}, u32[]{:S(2)}) collective-permute-start(f32[16,128]{1,0:T(8,128)S(1)} %get-tuple-element.32.refs_0_), channel_id=1, source_target_pairs={{0,4},{1,5},{2,6},{3,7},{4,0},{5,1},{6,2},{7,3},{8,12},{9,13},{10,... | collective-permute-start | bytes 24584 | tf_op jit(solution)/shard_map/ppermute | solution.py:340
  42.8 6.2 %collective-permute-start.13 = (f32[16,128]{1,0:T(8,128)S(1)}, f32[16,128]{1,0:T(8,128)S(1)}, u32[]{:S(2)}, u32[]{:S(2)}) collective-permute-start(f32[16,128]{1,0:T(8,128)S(1)} %shard_map.83.rest_0_), channel_id=1, source_target_pairs={{0,3},{1,2},{2,1},{3,0},{4,7},{5,6},{6,5},{7,4},{8,11},{9,10},{10,... | collective-permute-start | bytes 24584 | tf_op jit(solution)/shard_map/ppermute | solution.py:340
  42.9 7.9 %collective-permute-start.14 = (f32[16,128]{1,0:T(8,128)S(1)}, f32[16,128]{1,0:T(8,128)S(1)}, u32[]{:S(2)}, u32[]{:S(2)}) collective-permute-start(f32[16,128]{1,0:T(8,128)S(1)} %shard_map.83.rest_0_), channel_id=1, source_target_pairs={{0,2},{1,3},{2,0},{3,1},{4,6},{5,7},{6,4},{7,5},{8,10},{9,11},{10,... | collective-permute-start | bytes 24584 | tf_op jit(solution)/shard_map/ppermute | solution.py:340
  49.0 1.7 %collective-permute-start.15 = (f32[16,128]{1,0:T(8,128)S(1)}, f32[16,128]{1,0:T(8,128)S(1)}, u32[]{:S(2)}, u32[]{:S(2)}) collective-permute-start(f32[16,128]{1,0:T(8,128)S(1)} %shard_map.83.rest_0_), channel_id=1, source_target_pairs={{0,1},{1,0},{2,3},{3,2},{4,5},{5,4},{6,7},{7,6},{8,9},{9,8},{10,11... | collective-permute-start | bytes 24584 | tf_op jit(solution)/shard_map/ppermute | solution.py:340
  52.6 3.0 %collective-permute-start.16 = (f32[8,128]{1,0:T(8,128)S(1)}, f32[8,128]{1,0:T(8,128)S(1)}, u32[]{:S(2)}, u32[]{:S(2)}) collective-permute-start(f32[8,128]{1,0:T(8,128)S(1)} %get-tuple-element.34.refs_0_), channel_id=1, source_target_pairs={{0,3},{1,2},{2,1},{3,0},{4,7},{5,6},{6,5},{7,4},{8,11},{9,10},{10,... | collective-permute-start | bytes 12296 | tf_op jit(solution)/shard_map/ppermute | solution.py:340
  52.9 3.6 %collective-permute-start.17 = (f32[8,128]{1,0:T(8,128)S(1)}, f32[8,128]{1,0:T(8,128)S(1)}, u32[]{:S(2)}, u32[]{:S(2)}) collective-permute-start(f32[8,128]{1,0:T(8,128)S(1)} %get-tuple-element.34.refs_0_), channel_id=1, source_target_pairs={{0,2},{1,3},{2,0},{3,1},{4,6},{5,7},{6,4},{7,5},{8,10},{9,11},{10,... | collective-permute-start | bytes 12296 | tf_op jit(solution)/shard_map/ppermute | solution.py:340
  54.6 2.0 %collective-permute-start.18 = (f32[8,128]{1,0:T(8,128)S(1)}, f32[8,128]{1,0:T(8,128)S(1)}, u32[]{:S(2)}, u32[]{:S(2)}) collective-permute-start(f32[8,128]{1,0:T(8,128)S(1)} %get-tuple-element.34.refs_0_), channel_id=1, source_target_pairs={{0,1},{1,0},{2,3},{3,2},{4,5},{5,4},{6,7},{7,6},{8,9},{9,8},{10,11... | collective-permute-start | bytes 12296 | tf_op jit(solution)/shard_map/ppermute | solution.py:340
  56.5 6.3 %collective-permute-start.19 = (f32[8,128]{1,0:T(8,128)S(1)}, f32[8,128]{1,0:T(8,128)S(1)}, u32[]{:S(2)}, u32[]{:S(2)}) collective-permute-start(f32[8,128]{1,0:T(8,128)S(1)} %shard_map.85), channel_id=1, source_target_pairs={{0,12},{1,13},{2,14},{3,15},{4,8},{5,9},{6,10},{7,11},{8,4},{9,5},... | collective-permute-start | bytes 12296 | tf_op jit(solution)/shard_map/ppermute | solution.py:340
  58.8 4.5 %collective-permute-start.20 = (f32[8,128]{1,0:T(8,128)S(1)}, f32[8,128]{1,0:T(8,128)S(1)}, u32[]{:S(2)}, u32[]{:S(2)}) collective-permute-start(f32[8,128]{1,0:T(8,128)S(1)} %shard_map.85), channel_id=1, source_target_pairs={{0,8},{1,9},{2,10},{3,11},{4,12},{5,13},{6,14},{7,15},{8,0},{9,1},... | collective-permute-start | bytes 12296 | tf_op jit(solution)/shard_map/ppermute | solution.py:340
  59.1 4.2 %collective-permute-start.21 = (f32[8,128]{1,0:T(8,128)S(1)}, f32[8,128]{1,0:T(8,128)S(1)}, u32[]{:S(2)}, u32[]{:S(2)}) collective-permute-start(f32[8,128]{1,0:T(8,128)S(1)} %shard_map.85), channel_id=1, source_target_pairs={{0,4},{1,5},{2,6},{3,7},{4,0},{5,1},{6,2},{7,3},{8,12},{9,13},{10,... | collective-permute-start | bytes 12296 | tf_op jit(solution)/shard_map/ppermute | solution.py:340
